TPU v7x, 32 devices: a whole 2x2x4 slice. The times are simulated.
32 devices in a mesh: section: 4 (over x, core), wide: 2 (over y), narrow: 4 (over z).
Axes of the slice: x: 2, y: 2, z: 4, core: 2. Of those that a mesh axis runs over, the one named last changes fastest.
Arguments:
- valence_orbitals: float32 [8, 48, 2304], P(None, 'narrow'), may hold values from -6 to 6
- conduction_orbitals: float32 [8, 48, 2304], P(('section', 'wide'), 'narrow'), may hold values from -6 to 6
- valence_energy: float32 [8], replicated, may hold values from -7 to -1
- conduction_energy: float32 [8], replicated, may hold values from 1 to 7
- frequency: float32 [1], replicated, may hold values from 0.5 to 4
- pair_bands: int32 [32, 2], P(('section', 'wide')), may hold values from 0 to 7, as said below
- gvec_index: int32 [12288], replicated, may hold values from 0 to 110591, as said below
Outputs:
- chi: float32 [12288, 12288], P(('section', 'narrow'), 'wide')
Inputs may be any that keep to these rules, and one draw needn't show every extreme that they name: `pair_bands`: column 0 is a valence band, column 1 a conduction band; rows b * 4 to (b + 1) * 4 - 1 pair conduction band b with 4 distinct valence bands. `gvec_index`: the 12288 indices are distinct.
All inputs are finite; a program needn't handle non-finite values.
Results may differ from a plain program's by a relative error of at most 0.000094.
Values sent between devices are 32-bit elements; how exact they have to be, the bound alone decides.
No kernel may reach another device: no remote copies, remote signals or barrier semaphores. Data moves between devices by JAX's collectives and lax.ppermute only.
A program may use at most 192 MiB of HBM per device.

v0:
```python
import math

import jax
import jax.numpy as jnp
from jax import lax
from jax.sharding import PartitionSpec as P


def build_cosine(length):
    wavenumber = jnp.arange(length, dtype=jnp.float32)[:, None]
    position = jnp.arange(length, dtype=jnp.float32)[None, :]
    cosine = math.sqrt(2.0 / length) * jnp.cos(
        math.pi * (2.0 * position + 1.0) * wavenumber / (2.0 * length)
    )
    return jnp.where(wavenumber == 0.0, cosine * math.sqrt(0.5), cosine)


def contract(left_rows, right_rows):
    return lax.dot_general(
        left_rows,
        right_rows,
        (((0,), (0,)), ((), ())),
        precision=lax.Precision.HIGHEST,
        preferred_element_type=jnp.float32,
    )


def on_device(
    valence_orbitals,
    conduction_orbitals,
    valence_energy,
    conduction_energy,
    frequency,
    pair_bands,
    gvec_index,
):
    highest = lax.Precision.HIGHEST
    planes = valence_orbitals.shape[1]
    narrow_count = lax.axis_size("narrow")
    extent = planes * narrow_count
    pair_count = pair_bands.shape[0]
    section_count = lax.axis_size("section")
    wide_count = lax.axis_size("wide")
    total_pairs = pair_count * section_count * wide_count
    vector_count = gvec_index.shape[0]
    row_block = vector_count // (section_count * narrow_count)
    column_block = vector_count // wide_count
    cosine = build_cosine(extent)
    narrow_pos = lax.axis_index("narrow")
    local_table = lax.dynamic_slice_in_dim(cosine, narrow_pos * planes, planes, 1)
    band_offset = (
        lax.axis_index("section") * wide_count + lax.axis_index("wide")
    ) * conduction_orbitals.shape[0]
    local_band = pair_bands[:, 1] - band_offset
    valence_pick = valence_orbitals[pair_bands[:, 0]].reshape(pair_count, planes, extent, extent)
    conduction_pick = conduction_orbitals[local_band].reshape(pair_count, planes, extent, extent)
    density = valence_pick * conduction_pick
    sweep_one = jnp.einsum("pxyz,kz->pxyk", density, cosine, precision=highest)
    sweep_two = jnp.einsum("pxyk,jy->pxjk", sweep_one, cosine, precision=highest)
    sweep_three = jnp.einsum("pxjk,ix->pijk", sweep_two, local_table, precision=highest)
    partial_value = sweep_three.reshape(pair_count, -1)[:, gvec_index]
    energy_gap = conduction_energy[pair_bands[:, 1]] - valence_energy[pair_bands[:, 0]]
    weight = (
        -4.0
        * energy_gap
        / (energy_gap * energy_gap + frequency[0] * frequency[0])
        / math.sqrt(total_pairs)
    )
    own_rows = lax.psum_scatter(
        partial_value.reshape(pair_count, section_count, narrow_count, row_block),
        "narrow",
        scatter_dimension=2,
        tiled=True,
    )
    coefficients = lax.all_gather(own_rows, "narrow", axis=2, tiled=True).reshape(
        pair_count, vector_count
    )
    row_send = (own_rows * weight[:, None, None, None]).reshape(
        pair_count, section_count, row_block
    )
    row_recv = lax.all_to_all(row_send, "section", split_axis=1, concat_axis=0, tiled=True).reshape(
        section_count, pair_count, row_block
    )
    column_send = coefficients.reshape(pair_count, wide_count, column_block)
    column_recv = lax.all_to_all(
        column_send, "wide", split_axis=1, concat_axis=0, tiled=True
    ).reshape(wide_count * pair_count, column_block)
    rows_all = lax.all_gather(row_recv, "wide", axis=1, tiled=True).reshape(-1, row_block)
    return contract(rows_all, lax.all_gather(column_recv, "section", axis=0, tiled=True))


def solution(mesh):
    in_specs = (
        P(None, "narrow", None),
        P(("section", "wide"), "narrow", None),
        P(),
        P(),
        P(),
        P(("section", "wide"), None),
        P(),
    )
    out_specs = P(("section", "narrow"), "wide")
    return jax.shard_map(
        on_device, mesh=mesh, in_specs=in_specs, out_specs=out_specs, check_vma=False
    )
```

profile of v0, /device:TPU:0, one launch (start us, length us, event | category | flops | bytes accessed | tf_op | source)
XLA Modules:
  0.0 211.8 jit_solution(16049612886035854249)
XLA Ops:
  6.5 0.0 copy-start
  6.5 0.0 all-reduce.3.cloned.1.call-start
  6.6 0.8 fusion.11
  7.3 0.9 copy.49
  8.3 0.0 copy-done
  8.3 1.6 gather_fusion
  9.9 0.1 broadcast_multiply_fusion
  10.0 0.8 mul.129
  10.8 0.2 multiply_select_fusion
  11.0 1.2 fusion.1
  12.2 1.3 convolution_bitcast_fusion.1
  13.5 5.5 %convolution_bitcast_fusion = f32[4,48,48,48]{3,1,2,0:T(8,128)} fusion(f32[4,12,48,48]{3,2,1,0:T(8,128)S(1)} %convolution_bitcast_fusion.1, f32[48,48]{0,1:T(8,128)S(1)} %multiply_select_fusion, s32[]{:T(128)S(6)} %select_n.28), kind=kOutput, calls=%fused_computation.4 | convolution fusion | flops 63700992 | bytes 2957316 | tf_op jit(solution)/shard_map/pxjk,ix->pijk/dot_general | solution.py:60
  19.1 0.0 copy-start.4
  19.1 27.8 %copy.37 = f32[4,48,48,48]{0,3,2,1:T(8,128)} copy(f32[4,48,48,48]{3,1,2,0:T(8,128)} %convolution_bitcast_fusion) | data formatting | bytes 3538944 | tf_op jit(solution)/shard_map/reshape | solution.py:61
  46.9 0.0 copy-done.4
  46.9 58.6 %gather_fusion.1 = f32[12288,4]{1,0:T(8,128)} fusion(f32[4,110592]{0,1:T(8,128)} %bitcast.45, s32[12288]{0:T(1024)S(1)} %fusion.6), kind=kCustom, calls=%fused_computation.1 | custom fusion | bytes 442368 | tf_op jit(solution)/shard_map/gather | solution.py:61
  105.5 0.0 copy-start.2
  105.5 0.0 copy-start.3
  105.5 5.1 %copy.26 = f32[4,4,4,768]{3,0,1,2:T(4,128)} copy(f32[4,4,4,768]{0,3,2,1:T(8,128)} %bitcast.46) | data formatting | bytes 393216 | tf_op jit(solution)/shard_map/reshape | solution.py:70
  110.6 0.0 copy-start.5
  110.6 0.0 all-reduce.3.cloned.1.call-update
  110.7 0.0 copy-done.2
  110.7 0.6 gather_fusion.3
  112.0 0.0 copy-done.3
  112.0 0.6 gather_fusion.2
  112.6 0.0 copy-done.5
  112.6 0.7 dynamic-slice
  113.3 35.3 %all-reduce.3.cloned.1.call-done = f32[4,4,4,768]{3,0,1,2:T(4,128)} async-done(((f32[4,4,4,768]{3,0,1,2:T(4,128)}), f32[4,4,4,768]{3,0,1,2:T(4,128)}) %all-reduce.3.cloned.1.call-update) | async-done | bytes 196624
  148.6 2.2 %multiply_bitcast_fusion = (f32[4,4,768]{2,0,1:T(4,128)}, f32[4,4,1,768]{3,0,1,2:T(4,128)S(1)}) fusion(f32[4]{0:T(128)S(1)} %fusion.13, f32[4,4,4,768]{3,0,1,2:T(4,128)} %all-reduce.3.cloned.1.call-done, u32[]{:T(128)} %bitcast.20), kind=kLoop, calls=%fused_computation.16 | loop fusion | flops 12288 | bytes 147476 | tf_op jit(solution)/shard_map/reshape | solution.py:78
  150.8 3.3 %all-to-all-start = ((f32[4,4,768]{2,0,1:T(4,128)}), f32[4,4,768]{2,0,1:T(4,128)S(1)}, u32[]{:S(2)}, u32[]{:S(2)}) async-start(f32[4,4,768]{2,0,1:T(4,128)} %get-tuple-element.5), calls=%async_computation | async-start | bytes 98304 | tf_op jit(solution)/shard_map/all_to_all | solution.py:81
  154.1 13.6 %all_gather.10 = f32[4,4,4,768]{3,1,0,2:T(4,128)S(1)} all-gather(f32[4,4,1,768]{3,1,0,2:T(4,128)S(1)} %copy.29), channel_id=1, replica_groups=mesh['section'=4,'wide'=2,'narrow'=4] {'narrow'}, dimensions={2}, use_global_device_ids=true | all-gather | bytes 245760 | tf_op jit(solution)/shard_map/all_gather | solution.py:75
  167.7 0.1 copy.30
  167.8 0.2 reshape_reshape.3
  168.0 0.8 copy.31
  168.8 0.0 all-to-all-done
  168.8 3.4 %all-to-all-start.1 = ((f32[4,2,6144]{2,0,1:T(4,128)}), f32[4,2,6144]{2,0,1:T(4,128)S(1)}, u32[]{:S(2)}, u32[]{:S(2)}) async-start(f32[4,2,6144]{2,0,1:T(4,128)} %copy.31), calls=%async_computation.1 | async-start | bytes 393216 | tf_op jit(solution)/shard_map/all_to_all | solution.py:85
  172.3 5.3 %all-gather = f32[4,8,1,768]{3,0,2,1:T(4,128)S(1)} all-gather(f32[4,4,1,768]{3,0,2,1:T(4,128)S(1)} %copy.27), channel_id=2, replica_groups=mesh['section'=4,'wide'=2,'narrow'=4] {'wide'}, dimensions={1}, use_global_device_ids=true | all-gather | bytes 147456 | tf_op jit(solution)/shard_map/all_gather | solution.py:88
  177.6 0.0 all-to-all-done.1
  177.6 0.1 reshape.55
  177.7 9.2 %all_gather.11 = f32[32,6144]{1,0:T(8,128)S(1)} all-gather(f32[8,6144]{1,0:T(8,128)S(1)} %reshape.55), channel_id=1, replica_groups=mesh['section'=4,'wide'=2,'narrow'=4] {'section'}, dimensions={0}, use_global_device_ids=true | all-gather | bytes 983040 | tf_op jit(solution)/shard_map/all_gather | solution.py:89
  186.9 0.0 copy-start.1
  186.9 18.0 %fusion.3 = f32[768,6144]{1,0:T(8,128)} fusion(f32[32,6144]{1,0:T(8,128)S(1)} %all_gather.11, f32[4,8,1,768]{3,0,2,1:T(4,128)S(1)} %all-gather), kind=kOutput, calls=%fused_computation.12 | convolution fusion | flops 1811939328 | bytes 19759104 | tf_op jit(solution)/shard_map/dot_general | solution.py:19
  204.9 0.0 copy-done.1
  (7 shorter events, 0.1 us)
Async XLA Ops:
  6.5 1.7 copy-start
  6.5 142.1 %all-reduce.3.cloned.1.call-start = ((), (), s32[]{:S(2)}) async-start(), calls=%async_computation.2 | async-start | bytes 393216
  19.1 27.8 %copy-start.4 = (s32[12288]{0:T(1024)S(1)}, s32[12288]{0:T(1024)}, u32[]{:S(2)}) copy-start(s32[12288]{0:T(1024)} %param.13) | copy-start | bytes 147460
  105.5 5.2 %copy-start.2 = (f32[8]{0:T(128)S(1)}, f32[8]{0:T(128)}, u32[]{:S(2)}) copy-start(f32[8]{0:T(128)} %param.9) | copy-start | bytes 100
  105.5 6.5 %copy-start.3 = (f32[8]{0:T(128)S(1)}, f32[8]{0:T(128)}, u32[]{:S(2)}) copy-start(f32[8]{0:T(128)} %param.10) | copy-start | bytes 100
  110.6 2.0 copy-start.5
  150.8 18.1 %all-to-all-start = ((f32[4,4,768]{2,0,1:T(4,128)}), f32[4,4,768]{2,0,1:T(4,128)S(1)}, u32[]{:S(2)}, u32[]{:S(2)}) async-start(f32[4,4,768]{2,0,1:T(4,128)} %get-tuple-element.5), calls=%async_computation | async-start | bytes 98304 | tf_op jit(solution)/shard_map/all_to_all | solution.py:81
  168.8 8.8 %all-to-all-start.1 = ((f32[4,2,6144]{2,0,1:T(4,128)}), f32[4,2,6144]{2,0,1:T(4,128)S(1)}, u32[]{:S(2)}, u32[]{:S(2)}) async-start(f32[4,2,6144]{2,0,1:T(4,128)} %copy.31), calls=%async_computation.1 | async-start | bytes 393216 | tf_op jit(solution)/shard_map/all_to_all | solution.py:85
  186.9 18.0 %copy-start.1 = (f32[8,12,2304]{2,0,1:T(8,128)S(1)}, f32[8,12,2304]{2,0,1:T(8,128)}, u32[]{:S(2)}) copy-start(f32[8,12,2304]{2,0,1:T(8,128)} %param.7) | copy-start | bytes 2654212
Sparse Core Ops, SparseCore 0:
  110.8 37.7 all-reduce.2
where the time goes:
time: 213 us; the launch traced here: 212 us
  local copies, waits for them, and re-layouts  98 us (46%)
  waiting for transfers between devices  35.3 us (17%)
  blocking collectives  28.2 us (13%)
  matrix products  26.1 us (12%)
  between operations  14.2 us (7%)
  starting transfers between devices  6.72 us (3%)
  other arithmetic  3.28 us (2%)
    gather x1, local copies, waits for them, and re-layouts, on_device(): partial_value = sweep_three.reshape(pair_count, -1)[:, gvec_index]  58.6 us
    unnamed x2, waiting for transfers between devices  35.3 us
    reshape x1, local copies, waits for them, and re-layouts, on_device(): partial_value = sweep_three.reshape(pair_count, -1)[:, gvec_index]  27.8 us
    dot_general x1, matrix products, contract(): lax.dot_general(left_rows, right_rows, (((0,), (0,)), ((), ())), precisio...  18 us
    all_gather x1, blocking collectives, on_device(): lax.all_gather(own_rows, 'narrow', axis=2, tiled=True)  13.6 us
    all_gather x1, blocking collectives, on_device(): lax.all_gather(column_recv, 'section', axis=0, tiled=True)  9.21 us
    dot_general x1, matrix products, on_device(): jnp.einsum('pxjk,ix->pijk', sweep_two, local_table, precision=highest)  5.55 us
    all_gather x1, blocking collectives, on_device(): lax.all_gather(row_recv, 'wide', axis=1, tiled=True).reshape(-1, row_block)  5.31 us
  transfers between devices with their start and end apart: 3, of which 1 were waited for; matrix products, arithmetic and copies ran while one was open for 1% of the time, Pallas kernels for 0%

commit v1 on v0

v1 whole, which is shorter than its diff:
```python
import functools
import math

import jax
import jax.numpy as jnp
import numpy as np
from jax import lax
from jax.experimental import pallas as pl
from jax.experimental.pallas import tpu as pltpu
from jax.sharding import PartitionSpec as P

LANES = 128
ROWS = 8
F32 = jnp.float32
BF16 = jnp.bfloat16


def cosine_table(length):
    wavenumber = np.arange(length, dtype=np.float64)[:, None]
    position = np.arange(length, dtype=np.float64)[None, :]
    table = math.sqrt(2.0 / length) * np.cos(
        math.pi * (2.0 * position + 1.0) * wavenumber / (2.0 * length)
    )
    table[0] *= math.sqrt(0.5)
    return table.astype(np.float32)


def split(value):
    high = value.astype(BF16)
    low = (value - high.astype(F32)).astype(BF16)
    return high, low


def z_weights(cosine, per_chunk, slot):
    extent = cosine.shape[0]
    out = np.zeros((per_chunk * extent, per_chunk * slot), np.float32)
    for y in range(per_chunk):
        out[y * extent : (y + 1) * extent, y * slot : y * slot + extent] = cosine.T
    return out


def y_weights(cosine):
    extent = cosine.shape[0]
    half = cosine[:, : extent // 2].reshape(extent * extent // 4, 2)
    return np.repeat(half, LANES // 2, axis=1)


def x_tables(cosine, planes, pairs):
    extent = cosine.shape[0]
    out = np.zeros((extent // planes, planes * pairs, LANES), np.float32)
    for part in range(extent // planes):
        block = cosine[:, part * planes : (part + 1) * planes].T
        out[part, :, :extent] = np.repeat(block, pairs, axis=0)
    return out


def pick_blocks(extent, rows, pairs, count, block_of, index_ref, table_ref, scaled_ref, out_ref, lane_ref, chunk_ref, first_ref, basis_ref):
    tiles = rows // ROWS
    per_plane = extent * extent // LANES
    index = index_ref[...]
    lane_ref[...] = index & (LANES - 1)
    upper = index >> (LANES.bit_length() - 1)
    plane = (upper * ((1 << 16) // per_plane + 1)) >> 16
    first_ref[...] = plane
    chunk_ref[...] = upper - plane * per_plane
    for s in range(per_plane):
        high, low = split(table_ref[s])
        basis_ref[pl.ds(0, rows), pl.ds(s * LANES, LANES)] = high
        basis_ref[pl.ds(rows, rows), pl.ds(s * LANES, LANES)] = low
    take = functools.partial(jnp.take_along_axis, axis=1, mode="promise_in_bounds")
    wide = 2 * LANES
    steps = extent * extent // wide
    inside = lax.broadcasted_iota(jnp.int32, (wide, wide), 0).astype(F32).astype(BF16)
    one = jnp.ones((), BF16)
    zero = jnp.zeros((), BF16)

    def row_of(ref, b):
        return jnp.broadcast_to(ref[pl.ds(b, 1), :], (ROWS, LANES))

    def finish(q, b, picked):
        first = row_of(first_ref, b)
        out = None
        for t in range(tiles):
            term = picked[t] * take(scaled_ref[pl.ds(t * ROWS, ROWS), :], first)
            out = term if out is None else out + term
        out = out + pltpu.roll(out, pairs, 0)
        out_ref[q] = out[:pairs]

    def three(step, carry):
        places = [step * 3 + u for u in range(3)]
        ids = [block_of(q) for q in places]
        lane = jnp.concatenate([lane_ref[pl.ds(b, 1), :] for b in ids[:2]], axis=1)
        chunk = jnp.concatenate([chunk_ref[pl.ds(b, 1), :] for b in ids[:2]], axis=1)
        within = lane + (chunk & 1) * LANES
        tile = chunk >> 1
        total = jnp.zeros((2 * rows, wide), F32)
        third_lane, third_chunk = row_of(lane_ref, ids[2]), row_of(chunk_ref, ids[2])
        third = [None] * tiles
        for s in range(steps):
            key = jnp.where(tile == s, within, -1).astype(F32).astype(BF16)
            hot = jnp.where(inside == key, one, zero)
            total = total + jnp.dot(basis_ref[:, pl.ds(s * wide, wide)], hot, preferred_element_type=F32)
            for c in (2 * s, 2 * s + 1):
                for t in range(tiles):
                    found = take(table_ref[c, pl.ds(t * ROWS, ROWS), :], third_lane)
                    third[t] = found if c == 0 else jnp.where(third_chunk == c, found, third[t])
        picked = total[:rows] + total[rows:]
        for u in range(2):
            finish(places[u], ids[u], [picked[t * ROWS : (t + 1) * ROWS, u * LANES : (u + 1) * LANES] for t in range(tiles)])
        finish(places[2], ids[2], third)
        return carry

    lax.fori_loop(0, count // 3, three, 0, unroll=4)


def sweep_kernel(
    sizes,
    bands_ref,
    valence_energy_ref,
    conduction_energy_ref,
    frequency_ref,
    valence_ref,
    conduction_ref,
    z_high_ref,
    z_low_ref,
    y_ref,
    x_ref,
    index_ref,
    out_ref,
    table_ref,
    scaled_ref,
    density_ref,
    fold_ref,
    lane_ref,
    chunk_ref,
    first_ref,
    basis_ref,
):
    extent, planes, pairs, total_pairs, count, block_of = sizes
    rows = planes * pairs
    tiles = rows // ROWS
    per_chunk = 3 * LANES // extent
    groups = extent // per_chunk
    narrow_pos = lax.axis_index("narrow")
    band_offset = (lax.axis_index("section") * lax.axis_size("wide") + lax.axis_index("wide")) * conduction_ref.shape[0]
    for p in range(pairs):
        v = bands_ref[p, 0]
        c = bands_ref[p, 1] - band_offset
        for m in range(groups):
            for part in range(3):
                lanes = pl.ds((m * 3 + part) * LANES, LANES)
                density_ref[m, part, pl.ds(p, planes, stride=pairs), :] = valence_ref[v, :, lanes] * conduction_ref[c, :, lanes]
    density = jnp.concatenate([density_ref[:, part].reshape(groups * rows, LANES) for part in range(3)], axis=1)
    high, low = split(density)
    dot = functools.partial(jnp.dot, preferred_element_type=F32)
    swept = dot(high, z_high_ref[...]) + dot(low, z_high_ref[...]) + dot(high, z_low_ref[...])
    quarter = per_chunk // 2
    for m in range(groups // 2):
        for q in range(quarter):
            near = swept[m * rows : (m + 1) * rows, q * LANES : (q + 1) * LANES]
            far_m, far_q = groups - 1 - m, quarter - 1 - q
            far = swept[far_m * rows : (far_m + 1) * rows, far_q * LANES : (far_q + 1) * LANES]
            far = pltpu.roll(far, LANES // 2, 1)
            fold_ref[0, m * quarter + q] = near + far
            fold_ref[1, m * quarter + q] = near - far
    terms = extent // 4
    lane_id = lax.broadcasted_iota(jnp.int32, (ROWS, LANES), 1)

    def sweep_tile(t, carry):
        where_rows = pl.ds(pl.multiple_of(t * ROWS, ROWS), ROWS)
        parts = [[fold_ref[par, s, where_rows, :] for s in range(terms)] for par in range(2)]
        chunks = {}
        for j in range(extent):
            total = None
            for s in range(terms):
                term = parts[j % 2][s] * y_ref[pl.ds(j * terms + s, 1), :]
                total = term if total is None else total + term
            total = total + pltpu.roll(total, LANES // 2, 1)
            start = j * extent
            offset = start % LANES
            moved = total if offset % (LANES // 2) == 0 else pltpu.roll(total, offset, 1)
            for chunk in range(start // LANES, (start + extent - 1) // LANES + 1):
                begin = start - chunk * LANES
                chunks[chunk] = moved if begin <= 0 else jnp.where(lane_id >= begin, moved, chunks[chunk])
                if start + extent >= (chunk + 1) * LANES:
                    table_ref[chunk, where_rows, :] = chunks.pop(chunk)
        return carry

    lax.fori_loop(0, tiles, sweep_tile, 0)
    row_pair = lax.broadcasted_iota(jnp.int32, (ROWS, LANES), 0) % pairs
    gap = jnp.zeros((ROWS, LANES), F32)
    for p in range(pairs):
        one_gap = conduction_energy_ref[bands_ref[p, 1]] - valence_energy_ref[bands_ref[p, 0]]
        gap = jnp.where(row_pair == p, one_gap, gap)
    frequency = frequency_ref[0]
    scale = jnp.sqrt(4.0 * gap / (gap * gap + frequency * frequency) / math.sqrt(total_pairs))
    for t in range(tiles):
        scaled_ref[pl.ds(t * ROWS, ROWS), :] = x_ref[narrow_pos, pl.ds(t * ROWS, ROWS), :] * scale
    pick_blocks(extent, rows, pairs, count, block_of(), index_ref, table_ref, scaled_ref, out_ref, lane_ref, chunk_ref, first_ref, basis_ref)


def pick_kernel(sizes, index_ref, table_ref, scaled_ref, out_ref, lane_ref, chunk_ref, first_ref, basis_ref):
    extent, rows, pairs, count, block_of = sizes
    pick_blocks(extent, rows, pairs, count, block_of(), index_ref, table_ref, scaled_ref, out_ref, lane_ref, chunk_ref, first_ref, basis_ref)


def whole(shape):
    return pl.BlockSpec(shape, lambda i: (0,) * len(shape))


SMEM = pl.BlockSpec(memory_space=pltpu.SMEM)


def pick_scratch(blocks, rows, area):
    return [pltpu.VMEM((blocks, LANES), jnp.int32)] * 3 + [pltpu.VMEM((2 * rows, area), BF16)]


def sweep_call(bands, valence_energy, conduction_energy, frequency, valence, conduction, index, total_pairs, count, block_of):
    pairs = bands.shape[0]
    planes, area = valence.shape[1], valence.shape[2]
    extent = math.isqrt(area)
    rows = planes * pairs
    cosine = cosine_table(extent)
    per_chunk = 3 * LANES // extent
    groups = extent // per_chunk
    weights = z_weights(cosine, per_chunk, LANES // 2)
    z_high = weights.astype(BF16)
    z_low = (weights - z_high.astype(np.float32)).astype(BF16)
    operands = [valence, conduction, jnp.asarray(z_high), jnp.asarray(z_low)]
    operands += [jnp.asarray(y_weights(cosine)), jnp.asarray(x_tables(cosine, planes, pairs)), index]
    shapes = [(count, pairs, LANES), (area // LANES, rows, LANES), (rows, LANES)]
    return pl.pallas_call(
        functools.partial(sweep_kernel, (extent, planes, pairs, total_pairs, count, block_of)),
        grid=(1,),
        out_shape=[jax.ShapeDtypeStruct(shape, F32) for shape in shapes],
        in_specs=[SMEM] * 4 + [whole(a.shape) for a in operands],
        out_specs=[whole(shape) for shape in shapes],
        scratch_shapes=[
            pltpu.VMEM((groups, 3, rows, LANES), F32),
            pltpu.VMEM((2, extent // 4, rows, LANES), F32),
        ]
        + pick_scratch(index.shape[0], rows, area),
        cost_estimate=pl.CostEstimate(flops=8_000_000_000, bytes_accessed=4_000_000, transcendentals=0),
        name="sweep",
    )(bands, valence_energy, conduction_energy, frequency, *operands)


def pick_call(index, table, scaled, pairs, count, block_of):
    rows = table.shape[1]
    area = table.shape[0] * LANES
    return pl.pallas_call(
        functools.partial(pick_kernel, (math.isqrt(area), rows, pairs, count, block_of)),
        grid=(1,),
        out_shape=jax.ShapeDtypeStruct((count, pairs, LANES), F32),
        in_specs=[whole(a.shape) for a in (index, table, scaled)],
        out_specs=whole((count, pairs, LANES)),
        scratch_shapes=pick_scratch(index.shape[0], rows, area),
        cost_estimate=pl.CostEstimate(flops=4_000_000_000, bytes_accessed=1_000_000, transcendentals=0),
        name="pick",
    )(index, table, scaled)


def arrange_kernel(row_tiles, near_ref, far_ref, own_ref, wide_ref, narrow_ref, both_ref):
    narrow_count = lax.axis_size("narrow")
    half = narrow_count * row_tiles
    wide_pos, narrow_pos = lax.axis_index("wide"), lax.axis_index("narrow")
    for out_ref, w, n in (
        (own_ref, wide_pos, narrow_pos),
        (wide_ref, 1 - wide_pos, narrow_pos),
        (narrow_ref, wide_pos, narrow_pos ^ 1),
        (both_ref, 1 - wide_pos, narrow_pos ^ 1),
    ):
        columns = pl.ds(w * half, half)
        rows = pl.ds((1 - w) * half + n * row_tiles, row_tiles)
        out_ref[pl.ds(0, half)] = near_ref[columns] + far_ref[columns]
        out_ref[pl.ds(half, row_tiles)] = near_ref[rows] + far_ref[rows]


def arrange_call(near, far, row_tiles):
    blocks, pairs, _ = near.shape
    shape = (blocks // 2 + row_tiles, pairs, LANES)
    return pl.pallas_call(
        functools.partial(arrange_kernel, row_tiles),
        grid=(1,),
        out_shape=[jax.ShapeDtypeStruct(shape, F32)] * 4,
        in_specs=[whole(near.shape)] * 2,
        out_specs=[whole(shape)] * 4,
        name="arrange",
    )(near, far)


def stack_split(value, order):
    high, low = split(value)
    return jnp.concatenate([low if part else high for part in order], axis=0)


def product_kernel(row_tiles, pairs, own_ref, across_ref, core_ref, far_ref, out_ref, rows_ref, gather_ref):
    section, wide_pos, narrow_pos = lax.axis_index("section"), lax.axis_index("wide"), lax.axis_index("narrow")
    parity = narrow_pos & 1
    narrow_count = lax.axis_size("narrow")
    half = narrow_count * row_tiles
    sources = (own_ref, across_ref, core_ref, far_ref)

    def collect(kind, start):
        for i, ref in enumerate(sources):
            for b in range(2):
                rows = pl.ds((2 * i + b) * pairs, pairs)
                for r in range(row_tiles):
                    gather_ref[rows, pl.ds(r * LANES, LANES)] = ref[2 * kind + b, start + r]
        return gather_ref[...]

    step = pl.program_id(0)

    @pl.when(step == 0)
    def _():
        start = jnp.where(section // 2 == wide_pos, narrow_pos * row_tiles, half)
        value = collect((section & 1) ^ parity, start)
        high, low = split(-value)
        high, low = high.astype(F32), low.astype(F32)
        stacked = jnp.concatenate([high, high, low, low], axis=0)
        rows_ref[...] = stacked.T.astype(BF16)

    value = collect((step // narrow_count) ^ parity, (step % narrow_count) * row_tiles)
    out_ref[...] = jnp.dot(rows_ref[...], stack_split(value, (0, 1, 0, 1)), preferred_element_type=F32)


def product_call(sources, row_tiles):
    _, blocks, pairs, _ = sources[0].shape
    row_block = row_tiles * LANES
    narrow_count = blocks // row_tiles - 1
    depth = 2 * len(sources) * pairs
    return pl.pallas_call(
        functools.partial(product_kernel, row_tiles, pairs),
        grid=(2 * narrow_count,),
        out_shape=jax.ShapeDtypeStruct((row_block, 2 * narrow_count * row_block), F32),
        in_specs=[whole(a.shape) for a in sources],
        out_specs=pl.BlockSpec((row_block, row_block), lambda i: (0, i)),
        scratch_shapes=[pltpu.VMEM((row_block, 4 * depth), BF16), pltpu.VMEM((depth, row_block), F32)],
        name="product",
    )(*sources)


def contract(left_rows, right_rows):
    return lax.dot_general(
        left_rows,
        right_rows,
        (((0,), (0,)), ((), ())),
        precision=lax.Precision.HIGHEST,
        preferred_element_type=F32,
    )


def on_device(valence, conduction, valence_energy, conduction_energy, frequency, pair_bands, gvec_index):
    pairs = pair_bands.shape[0]
    section_count, wide_count, narrow_count = (lax.axis_size(name) for name in ("section", "wide", "narrow"))
    total_pairs = pairs * section_count * wide_count
    vector_count = gvec_index.shape[0]
    row_block = vector_count // (section_count * narrow_count)
    column_block = vector_count // wide_count
    row_tiles = row_block // LANES
    blocks = vector_count // LANES
    index = gvec_index.reshape(blocks, LANES)
    sweep = functools.partial(sweep_call, pair_bands, valence_energy, conduction_energy, frequency, valence, conduction, index, total_pairs)

    if not (section_count == 4 and wide_count == 2 and narrow_count == 4):
        partial_value = sweep(blocks, lambda: lambda q: q)[0]
        partial_value = jnp.swapaxes(partial_value, 0, 1).reshape(pairs, section_count, narrow_count, row_block)
        own_rows = lax.psum_scatter(partial_value, "narrow", scatter_dimension=2, tiled=True)
        coefficients = lax.all_gather(own_rows, "narrow", axis=2, tiled=True).reshape(pairs, vector_count)
        row_send = own_rows.reshape(pairs, section_count, row_block)
        row_recv = lax.all_to_all(row_send, "section", split_axis=1, concat_axis=0, tiled=True)
        row_recv = row_recv.reshape(section_count, pairs, row_block)
        column_send = coefficients.reshape(pairs, wide_count, column_block)
        column_recv = lax.all_to_all(column_send, "wide", split_axis=1, concat_axis=0, tiled=True)
        column_recv = column_recv.reshape(wide_count * pairs, column_block)
        rows_all = lax.all_gather(row_recv, "wide", axis=1, tiled=True).reshape(-1, row_block)
        return contract(-rows_all, lax.all_gather(column_recv, "section", axis=0, tiled=True))

    half = narrow_count * row_tiles

    def block_of(other):
        def make():
            own = (lax.axis_index("narrow") & 1) ^ other
            return lambda q: q + (q // half + own) * half

        return make

    away, table, scaled = sweep(blocks // 2, block_of(1))
    kept = pick_call(index, table, scaled, pairs, blocks // 2, block_of(0))
    flip = lambda bit: [(i, i ^ bit) for i in range(4)]
    summed = kept + lax.ppermute(away, "narrow", flip(1))
    opposite = lax.ppermute(summed, "narrow", flip(2))
    own, to_wide, to_narrow, to_both = arrange_call(summed, opposite, row_tiles)
    from_wide = lax.ppermute(to_wide, "wide", [(0, 1), (1, 0)])
    from_narrow = lax.ppermute(to_narrow, "narrow", flip(1))
    from_both = lax.ppermute(to_both, ("wide", "narrow"), [(i, i ^ 5) for i in range(8)])
    near = jnp.stack([own, from_wide, from_narrow, from_both])
    across = lax.ppermute(near, "section", flip(2))
    core = lax.ppermute(near, "section", flip(1))
    far = lax.ppermute(across, "section", flip(1))
    return product_call((near, across, core, far), row_tiles)


def solution(mesh):
    in_specs = (
        P(None, "narrow", None),
        P(("section", "wide"), "narrow", None),
        P(),
        P(),
        P(),
        P(("section", "wide"), None),
        P(),
    )
    out_specs = P(("section", "narrow"), "wide")
    return jax.shard_map(on_device, mesh=mesh, in_specs=in_specs, out_specs=out_specs, check_vma=False)
```

time: 213 us -> 59.5 us (0.28)
  local copies, waits for them, and re-layouts: 98 us -> 6.71 us
  blocking collectives: 28.2 us -> 0 us
  matrix products: 26.1 us -> 0 us
  Pallas kernels: 0 us -> 24.9 us
  waiting for transfers between devices: 35.3 us -> 14.3 us
  between operations: 14.2 us -> 0.71 us
  starting transfers between devices: 6.72 us -> 10.7 us
    gather x4 -> x0, local copies, waits for them, and re-layouts: 61.5 us -> none  [the longest x1 58.6 us: on_device(): partial_value = sweep_three.reshape(pair_count, -1)[:, gvec_index]]
    unnamed x2 -> x0, waiting for transfers between devices: 35.3 us -> none
    reshape x3 -> x0, local copies, waits for them, and re-layouts: 33 us -> none  [the longest x1 27.8 us: on_device(): partial_value = sweep_three.reshape(pair_count, -1)[:, gvec_index]]
    all_gather x3 -> x0, blocking collectives: 28.2 us -> none  [the longest x1 13.6 us: on_device(): lax.all_gather(own_rows, 'narrow', axis=2, tiled=True)]
    dot_general x4 -> x0, matrix products: 26.1 us -> none  [the longest x1 18 us: contract(): lax.dot_general(left_rows, right_rows, (((0,), (0,)), ((), ())), precisio...]
    pallas_call x0 -> x4, Pallas kernels: none -> 24.9 us  [the longest x1 9.74 us: product_call(): pl.pallas_call(functools.partial(product_kernel, row_tiles, pairs), grid=...]
    ppermute x0 -> x8, waiting for transfers between devices: none -> 14.3 us  [the longest x1 4.88 us: on_device(): across = lax.ppermute(near, 'section', flip(2))]
    ppermute x0 -> x8, starting transfers between devices: none -> 10.7 us  [the longest x1 3.04 us: on_device(): summed = kept + lax.ppermute(away, 'narrow', flip(1))]
  transfers between devices with their start and end apart: 3 -> 8, of which waited for: 1 -> 6; matrix products, arithmetic and copies ran while one was open for 1% -> 0% of each run, Pallas kernels for 0% -> 9%
where the time goes in v1:
time: 59.5 us; the launch traced here: 59.1 us
  Pallas kernels  24.9 us (42%)
  waiting for transfers between devices  14.3 us (24%)
  starting transfers between devices  10.7 us (18%)
  local copies, waits for them, and re-layouts  6.71 us (11%)
  other arithmetic  1.81 us (3%)
  between operations  0.71 us (1%)
    pallas_call x1, Pallas kernels, product_call(): pl.pallas_call(functools.partial(product_kernel, row_tiles, pairs), grid=...  9.74 us
    pallas_call x1, Pallas kernels, sweep_call(): pl.pallas_call(functools.partial(sweep_kernel, (extent, planes, pairs, to...  8.35 us
    unnamed x15, local copies, waits for them, and re-layouts  6.71 us
    pallas_call x1, Pallas kernels, pick_call(): pl.pallas_call(functools.partial(pick_kernel, (math.isqrt(area), rows, pa...  5.12 us
    ppermute x1, waiting for transfers between devices, on_device(): across = lax.ppermute(near, 'section', flip(2))  4.88 us
    ppermute x1, waiting for transfers between devices, on_device(): opposite = lax.ppermute(summed, 'narrow', flip(2))  4.5 us
    ppermute x1, starting transfers between devices, on_device(): summed = kept + lax.ppermute(away, 'narrow', flip(1))  3.04 us
    ppermute x1, starting transfers between devices, on_device(): opposite = lax.ppermute(summed, 'narrow', flip(2))  2.66 us
  transfers between devices with their start and end apart: 8, of which 6 were waited for; matrix products, arithmetic and copies ran while one was open for 0% of the time, Pallas kernels for 9%

profile of v1, /device:TPU:0, one launch (start us, length us, event | category | flops | bytes accessed | tf_op | source)
XLA Modules:
  0.0 59.1 jit_solution(17082024330735635213)
XLA Ops:
  0.7 1.3 %copy.12.bands_ref = s32[4,2]{1,0:T(4,128)} copy(s32[4,2]{0,1:T(2,128)} %param.16) | data formatting | bytes 64 | tf_op args[5]
  2.0 1.6 %copy.14.conduction_ref = f32[1,12,2304]{2,1,0:T(8,128)} copy(f32[1,12,2304]{2,0,1:T(1,128)} %param.12) | data formatting | bytes 221184 | tf_op args[1]
  3.5 2.5 %copy.13.valence_ref = f32[8,12,2304]{2,1,0:T(8,128)} copy(f32[8,12,2304]{2,0,1:T(8,128)} %param.11) | data formatting | bytes 1769472 | tf_op args[0]
  6.0 8.3 %sweep.1 = (f32[48,4,128]{2,1,0:T(4,128)}, f32[18,48,128]{2,1,0:T(8,128)}, f32[48,128]{1,0:T(8,128)}) custom-call(s32[4,2]{1,0:T(4,128)} %copy.12.bands_ref, f32[8]{0:T(128)} %valence_energy_ref.1, f32[8]{0:T(128)} %conduction_energy_ref.1, f32[1]{0:T(128)S(6)} %copy.15.frequency_ref, f32[8,12,2304]{2,1,0:T(8,128)} %copy.13.valence_ref, ...), custom_call_target="tpu_custom_call" | custom-call | flops 8000000000 | bytes 4000000 | tf_op jit(solution)/shard_map/sweep/pallas_call | solution.py:232
  14.4 3.0 %collective-permute-start = (f32[48,4,128]{2,1,0:T(4,128)}, f32[48,4,128]{2,1,0:T(4,128)S(1)}, u32[]{:S(2)}, u32[]{:S(2)}) collective-permute-start(f32[48,4,128]{2,1,0:T(4,128)} %get-tuple-element.14), channel_id=1, source_target_pairs={{0,1},{1,0},{2,3},{3,2},{4,5},{5,4},{6,7},{7,6},{8,9},{9,8},{10,11... | collective-permute-start | bytes 294920 | tf_op jit(solution)/shard_map/ppermute | solution.py:391
  17.4 5.1 %pick.1 = f32[48,4,128]{2,1,0:T(4,128)} custom-call(s32[96,128]{1,0:T(8,128)} %bitcast.10, f32[18,48,128]{2,1,0:T(8,128)} %get-tuple-element.12.table_ref, f32[48,128]{1,0:T(8,128)} %get-tuple-element.13.scaled_ref), custom_call_target="tpu_custom_call" | custom-call | flops 4000000000 | bytes 1000000 | tf_op jit(solution)/shard_map/pick/pallas_call | solution.py:251
  22.5 0.0 collective-permute-done
  22.5 0.9 %add.3.near_ref = f32[48,4,128]{2,1,0:T(4,128)S(1)} add(f32[48,4,128]{2,1,0:T(4,128)} %pick.1, f32[48,4,128]{2,1,0:T(4,128)S(1)} %collective-permute-done) | non-fusion elementwise | flops 24576 | bytes 294912 | tf_op jit(solution)/shard_map/add | solution.py:391
  23.4 0.0 copy-start.1
  23.5 2.7 %collective-permute-start.1 = (f32[48,4,128]{2,1,0:T(4,128)S(1)}, f32[48,4,128]{2,1,0:T(4,128)S(1)}, u32[]{:S(2)}, u32[]{:S(2)}) collective-permute-start(f32[48,4,128]{2,1,0:T(4,128)S(1)} %add.3.near_ref), channel_id=1, source_target_pairs={{0,2},{1,3},{2,0},{3,1},{4,6},{5,7},{6,4},{7,5},{8,10},{9,11},{10,... | collective-permute-start | bytes 294920 | tf_op jit(solution)/shard_map/ppermute | solution.py:392
  26.1 4.5 %collective-permute-done.1.far_ref = f32[48,4,128]{2,1,0:T(4,128)S(1)} collective-permute-done((f32[48,4,128]{2,1,0:T(4,128)S(1)}, f32[48,4,128]{2,1,0:T(4,128)S(1)}, u32[]{:S(2)}, u32[]{:S(2)}) %collective-permute-start.1) | collective-permute-done | bytes 98336 | tf_op jit(solution)/shard_map/ppermute | solution.py:392
  30.6 0.0 copy-done.1
  30.6 0.0 copy-start.5
  30.6 0.6 %copy-done.5 = f32[48,4,128]{2,1,0:T(4,128)} copy-done((f32[48,4,128]{2,1,0:T(4,128)}, f32[48,4,128]{2,1,0:T(4,128)S(1)}, u32[]{:S(2)}) %copy-start.5) | copy-done | bytes 98328
  31.3 1.7 %arrange.1 = (f32[30,4,128]{2,1,0:T(4,128)}, f32[30,4,128]{2,1,0:T(4,128)}, f32[30,4,128]{2,1,0:T(4,128)}, f32[30,4,128]{2,1,0:T(4,128)}) custom-call(f32[48,4,128]{2,1,0:T(4,128)} %copy-done.1, f32[48,4,128]{2,1,0:T(4,128)} %copy-done.5), custom_call_target="tpu_custom_call" | custom-call | tf_op jit(solution)/shard_map/arrange/pallas_call | solution.py:282
  33.0 1.6 %collective-permute-start.2 = (f32[30,4,128]{2,1,0:T(4,128)}, f32[30,4,128]{2,1,0:T(4,128)S(1)}, u32[]{:S(2)}, u32[]{:S(2)}) collective-permute-start(f32[30,4,128]{2,1,0:T(4,128)} %get-tuple-element.16), channel_id=1, source_target_pairs={{0,4},{4,0},{1,5},{5,1},{2,6},{6,2},{3,7},{7,3},{8,12},{12,8},{9,1... | collective-permute-start | bytes 184328 | tf_op jit(solution)/shard_map/ppermute | solution.py:394
  34.5 0.0 collective-permute-start.3
  34.5 1.9 %collective-permute-start.4 = (f32[30,4,128]{2,1,0:T(4,128)}, f32[30,4,128]{2,1,0:T(4,128)S(1)}, u32[]{:S(2)}, u32[]{:S(2)}) collective-permute-start(f32[30,4,128]{2,1,0:T(4,128)} %get-tuple-element.18), channel_id=1, source_target_pairs={{0,5},{1,4},{2,7},{3,6},{4,1},{5,0},{6,3},{7,2},{8,13},{9,12},{10,... | collective-permute-start | bytes 184328 | tf_op jit(solution)/shard_map/ppermute | solution.py:396
  36.4 0.9 %collective-permute-done.2 = f32[30,4,128]{2,1,0:T(4,128)S(1)} collective-permute-done((f32[30,4,128]{2,1,0:T(4,128)}, f32[30,4,128]{2,1,0:T(4,128)S(1)}, u32[]{:S(2)}, u32[]{:S(2)}) %collective-permute-start.2) | collective-permute-done | bytes 61472 | tf_op jit(solution)/shard_map/ppermute | solution.py:394
  37.4 1.6 %collective-permute-done.3 = f32[30,4,128]{2,1,0:T(4,128)S(1)} collective-permute-done((f32[30,4,128]{2,1,0:T(4,128)}, f32[30,4,128]{2,1,0:T(4,128)S(1)}, u32[]{:S(2)}, u32[]{:S(2)}) %collective-permute-start.3) | collective-permute-done | bytes 61472 | tf_op jit(solution)/shard_map/ppermute | solution.py:395
  39.0 0.9 %collective-permute-done.4 = f32[30,4,128]{2,1,0:T(4,128)S(1)} collective-permute-done((f32[30,4,128]{2,1,0:T(4,128)}, f32[30,4,128]{2,1,0:T(4,128)S(1)}, u32[]{:S(2)}, u32[]{:S(2)}) %collective-permute-start.4) | collective-permute-done | bytes 61472 | tf_op jit(solution)/shard_map/ppermute | solution.py:396
  39.9 0.9 %pad_maximum_fusion.own_ref = f32[4,30,4,128]{3,2,1,0:T(4,128)S(1)} fusion(f32[1,30,4,128]{3,2,1,0:T(4,128)S(1)} %bitcast.8, f32[1,30,4,128]{3,2,1,0:T(4,128)S(1)} %bitcast.7, f32[1,30,4,128]{3,2,1,0:T(4,128)S(1)} %bitcast.6, f32[1,30,4,128]{3,2,1,0:T(4,128)} %bitcast.5), kind=kLoop, calls=%fused_computation | loop fusion | flops 184320 | bytes 491520 | tf_op jit(solution)/shard_map/stack | solution.py:397
  40.8 0.0 copy-start
  40.8 1.5 %collective-permute-start.5 = (f32[4,30,4,128]{3,2,1,0:T(4,128)S(1)}, f32[4,30,4,128]{3,2,1,0:T(4,128)S(1)}, u32[]{:S(2)}, u32[]{:S(2)}) collective-permute-start(f32[4,30,4,128]{3,2,1,0:T(4,128)S(1)} %pad_maximum_fusion.own_ref), channel_id=1, source_target_pairs={{0,16},{8,24},{16,0},{24,8},{1,17},{9,25},{17,1},{25,9},{2,18},{10... | collective-permute-start | bytes 737288 | tf_op jit(solution)/shard_map/ppermute | solution.py:398
  42.3 0.0 collective-permute-start.6
  42.3 4.9 %collective-permute-done.5.across_ref = f32[4,30,4,128]{3,2,1,0:T(4,128)S(1)} collective-permute-done((f32[4,30,4,128]{3,2,1,0:T(4,128)S(1)}, f32[4,30,4,128]{3,2,1,0:T(4,128)S(1)}, u32[]{:S(2)}, u32[]{:S(2)}) %collective-permute-start.5) | collective-permute-done | bytes 245792 | tf_op jit(solution)/shard_map/ppermute | solution.py:398
  47.2 0.0 copy-start.2
  47.2 0.0 collective-permute-start.7
  47.2 0.0 collective-permute-done.6.core_ref
  47.2 0.0 copy-start.3
  47.2 1.5 %collective-permute-done.7.far_ref = f32[4,30,4,128]{3,2,1,0:T(4,128)S(1)} collective-permute-done((f32[4,30,4,128]{3,2,1,0:T(4,128)S(1)}, f32[4,30,4,128]{3,2,1,0:T(4,128)S(1)}, u32[]{:S(2)}, u32[]{:S(2)}) %collective-permute-start.7) | collective-permute-done | bytes 245792 | tf_op jit(solution)/shard_map/ppermute | solution.py:400
  48.7 0.0 copy-done
  48.7 0.0 copy-done.2
  48.7 0.0 copy-done.3
  48.7 0.0 copy-start.4
  48.7 0.7 %copy-done.4 = f32[4,30,4,128]{3,2,1,0:T(4,128)} copy-done((f32[4,30,4,128]{3,2,1,0:T(4,128)}, f32[4,30,4,128]{3,2,1,0:T(4,128)S(1)}, u32[]{:S(2)}) %copy-start.4) | copy-done | bytes 245784
  49.4 9.7 %product.1 = f32[768,6144]{1,0:T(8,128)} custom-call(f32[4,30,4,128]{3,2,1,0:T(4,128)} %copy-done, f32[4,30,4,128]{3,2,1,0:T(4,128)} %copy-done.2, f32[4,30,4,128]{3,2,1,0:T(4,128)} %copy-done.3, f32[4,30,4,128]{3,2,1,0:T(4,128)} %copy-done.4), custom_call_target="tpu_custom_call" | custom-call | tf_op jit(solution)/shard_map/product/pallas_call | solution.py:332
Async XLA Ops:
  14.4 8.2 %collective-permute-start = (f32[48,4,128]{2,1,0:T(4,128)}, f32[48,4,128]{2,1,0:T(4,128)S(1)}, u32[]{:S(2)}, u32[]{:S(2)}) collective-permute-start(f32[48,4,128]{2,1,0:T(4,128)} %get-tuple-element.14), channel_id=1, source_target_pairs={{0,1},{1,0},{2,3},{3,2},{4,5},{5,4},{6,7},{7,6},{8,9},{9,8},{10,11... | collective-permute-start | bytes 294920 | tf_op jit(solution)/shard_map/ppermute | solution.py:391
  23.4 7.2 %copy-start.1 = (f32[48,4,128]{2,1,0:T(4,128)}, f32[48,4,128]{2,1,0:T(4,128)S(1)}, u32[]{:S(2)}) copy-start(f32[48,4,128]{2,1,0:T(4,128)S(1)} %add.3.near_ref) | copy-start | bytes 294916
  23.5 7.2 %collective-permute-start.1 = (f32[48,4,128]{2,1,0:T(4,128)S(1)}, f32[48,4,128]{2,1,0:T(4,128)S(1)}, u32[]{:S(2)}, u32[]{:S(2)}) collective-permute-start(f32[48,4,128]{2,1,0:T(4,128)S(1)} %add.3.near_ref), channel_id=1, source_target_pairs={{0,2},{1,3},{2,0},{3,1},{4,6},{5,7},{6,4},{7,5},{8,10},{9,11},{10,... | collective-permute-start | bytes 294920 | tf_op jit(solution)/shard_map/ppermute | solution.py:392
  30.6 0.6 %copy-start.5 = (f32[48,4,128]{2,1,0:T(4,128)}, f32[48,4,128]{2,1,0:T(4,128)S(1)}, u32[]{:S(2)}) copy-start(f32[48,4,128]{2,1,0:T(4,128)S(1)} %collective-permute-done.1.far_ref) | copy-start | bytes 294916
  33.0 4.4 %collective-permute-start.2 = (f32[30,4,128]{2,1,0:T(4,128)}, f32[30,4,128]{2,1,0:T(4,128)S(1)}, u32[]{:S(2)}, u32[]{:S(2)}) collective-permute-start(f32[30,4,128]{2,1,0:T(4,128)} %get-tuple-element.16), channel_id=1, source_target_pairs={{0,4},{4,0},{1,5},{5,1},{2,6},{6,2},{3,7},{7,3},{8,12},{12,8},{9,1... | collective-permute-start | bytes 184328 | tf_op jit(solution)/shard_map/ppermute | solution.py:394
  34.5 4.4 %collective-permute-start.3 = (f32[30,4,128]{2,1,0:T(4,128)}, f32[30,4,128]{2,1,0:T(4,128)S(1)}, u32[]{:S(2)}, u32[]{:S(2)}) collective-permute-start(f32[30,4,128]{2,1,0:T(4,128)} %get-tuple-element.17), channel_id=1, source_target_pairs={{0,1},{1,0},{2,3},{3,2},{4,5},{5,4},{6,7},{7,6},{8,9},{9,8},{10,11... | collective-permute-start | bytes 184328 | tf_op jit(solution)/shard_map/ppermute | solution.py:395
  34.5 5.3 %collective-permute-start.4 = (f32[30,4,128]{2,1,0:T(4,128)}, f32[30,4,128]{2,1,0:T(4,128)S(1)}, u32[]{:S(2)}, u32[]{:S(2)}) collective-permute-start(f32[30,4,128]{2,1,0:T(4,128)} %get-tuple-element.18), channel_id=1, source_target_pairs={{0,5},{1,4},{2,7},{3,6},{4,1},{5,0},{6,3},{7,2},{8,13},{9,12},{10,... | collective-permute-start | bytes 184328 | tf_op jit(solution)/shard_map/ppermute | solution.py:396
  40.8 8.0 %copy-start = (f32[4,30,4,128]{3,2,1,0:T(4,128)}, f32[4,30,4,128]{3,2,1,0:T(4,128)S(1)}, u32[]{:S(2)}) copy-start(f32[4,30,4,128]{3,2,1,0:T(4,128)S(1)} %pad_maximum_fusion.own_ref) | copy-start | bytes 737284
  40.8 6.4 %collective-permute-start.5 = (f32[4,30,4,128]{3,2,1,0:T(4,128)S(1)}, f32[4,30,4,128]{3,2,1,0:T(4,128)S(1)}, u32[]{:S(2)}, u32[]{:S(2)}) collective-permute-start(f32[4,30,4,128]{3,2,1,0:T(4,128)S(1)} %pad_maximum_fusion.own_ref), channel_id=1, source_target_pairs={{0,16},{8,24},{16,0},{24,8},{1,17},{9,25},{17,1},{25,9},{2,18},{10... | collective-permute-start | bytes 737288 | tf_op jit(solution)/shard_map/ppermute | solution.py:398
  42.3 4.9 %collective-permute-start.6 = (f32[4,30,4,128]{3,2,1,0:T(4,128)S(1)}, f32[4,30,4,128]{3,2,1,0:T(4,128)S(1)}, u32[]{:S(2)}, u32[]{:S(2)}) collective-permute-start(f32[4,30,4,128]{3,2,1,0:T(4,128)S(1)} %pad_maximum_fusion.own_ref), channel_id=1, source_target_pairs={{0,8},{8,0},{16,24},{24,16},{1,9},{9,1},{17,25},{25,17},{2,10},{10... | collective-permute-start | bytes 737288 | tf_op jit(solution)/shard_map/ppermute | solution.py:399
  47.2 1.5 %copy-start.2 = (f32[4,30,4,128]{3,2,1,0:T(4,128)}, f32[4,30,4,128]{3,2,1,0:T(4,128)S(1)}, u32[]{:S(2)}) copy-start(f32[4,30,4,128]{3,2,1,0:T(4,128)S(1)} %collective-permute-done.5.across_ref) | copy-start | bytes 737284
  47.2 1.5 %collective-permute-start.7 = (f32[4,30,4,128]{3,2,1,0:T(4,128)S(1)}, f32[4,30,4,128]{3,2,1,0:T(4,128)S(1)}, u32[]{:S(2)}, u32[]{:S(2)}) collective-permute-start(f32[4,30,4,128]{3,2,1,0:T(4,128)S(1)} %collective-permute-done.5.across_ref), channel_id=1, source_target_pairs={{0,8},{8,0},{16,24},{24,16},{1,9},{9,1},{17,25},{25,17},{2,10},{10... | collective-permute-start | bytes 737288 | tf_op jit(solution)/shard_map/ppermute | solution.py:400
  47.2 1.5 %copy-start.3 = (f32[4,30,4,128]{3,2,1,0:T(4,128)}, f32[4,30,4,128]{3,2,1,0:T(4,128)S(1)}, u32[]{:S(2)}) copy-start(f32[4,30,4,128]{3,2,1,0:T(4,128)S(1)} %collective-permute-done.6.core_ref) | copy-start | bytes 737284
  48.7 0.7 %copy-start.4 = (f32[4,30,4,128]{3,2,1,0:T(4,128)}, f32[4,30,4,128]{3,2,1,0:T(4,128)S(1)}, u32[]{:S(2)}) copy-start(f32[4,30,4,128]{3,2,1,0:T(4,128)S(1)} %collective-permute-done.7.far_ref) | copy-start | bytes 737284

commit v2 on v1

v2 whole, which is shorter than its diff:
```python
import functools
import math

import jax
import jax.numpy as jnp
import numpy as np
from jax import lax
from jax.experimental import pallas as pl
from jax.experimental.pallas import tpu as pltpu
from jax.sharding import PartitionSpec as P

LANES = 128
ROWS = 8
F32 = jnp.float32
BF16 = jnp.bfloat16


def cosine_table(length):
    wavenumber = np.arange(length, dtype=np.float64)[:, None]
    position = np.arange(length, dtype=np.float64)[None, :]
    table = math.sqrt(2.0 / length) * np.cos(
        math.pi * (2.0 * position + 1.0) * wavenumber / (2.0 * length)
    )
    table[0] *= math.sqrt(0.5)
    return table.astype(np.float32)


def split(value):
    high = value.astype(BF16)
    low = (value - high.astype(F32)).astype(BF16)
    return high, low


def z_weights(cosine, per_chunk, slot):
    extent = cosine.shape[0]
    out = np.zeros((per_chunk * extent, per_chunk * slot), np.float32)
    for y in range(per_chunk):
        out[y * extent : (y + 1) * extent, y * slot : y * slot + extent] = cosine.T
    return out


def y_weights(cosine):
    extent = cosine.shape[0]
    half = cosine[:, : extent // 2].reshape(extent * extent // 4, 2)
    return np.repeat(half, LANES // 2, axis=1)


def x_tables(cosine, planes, pairs):
    extent = cosine.shape[0]
    out = np.zeros((extent // planes, planes * pairs, LANES), np.float32)
    for part in range(extent // planes):
        block = cosine[:, part * planes : (part + 1) * planes].T
        out[part, :, :extent] = np.repeat(block, pairs, axis=0)
    return out


def pick_blocks(pairs, count, block_of, index_ref, table_ref, scaled_ref, out_ref, basis_ref, lane_ref, chunk_ref, first_ref):
    per_plane, rows, _ = table_ref.shape
    tiles = rows // ROWS
    for s in range(per_plane):
        high, low = split(table_ref[s])
        basis_ref[pl.ds(s * rows, rows), pl.ds(0, LANES)] = high
        basis_ref[pl.ds(s * rows, rows), pl.ds(LANES, LANES)] = low
    index = index_ref[...]
    lane_ref[...] = index & (LANES - 1)
    upper = index >> (LANES.bit_length() - 1)
    plane = (upper * ((1 << 16) // per_plane + 1)) >> 16
    first_ref[...] = plane
    chunk_ref[...] = upper - plane * per_plane
    take = functools.partial(jnp.take_along_axis, axis=1, mode="promise_in_bounds")
    wide = 2 * LANES
    inside = lax.broadcasted_iota(jnp.int32, (LANES, wide), 0).astype(F32).astype(BF16)
    one = jnp.ones((), BF16)
    zero = jnp.zeros((), BF16)

    def row_of(ref, b):
        return jnp.broadcast_to(ref[pl.ds(b, 1), :], (ROWS, LANES))

    def select(chunk, candidate):
        picked = [None] * tiles
        for c in range(per_plane):
            mine = chunk == c
            for t in range(tiles):
                found = candidate(c, t)
                picked[t] = found if c == 0 else jnp.where(mine, found, picked[t])
        return picked

    def finish(q, b, picked):
        first = row_of(first_ref, b)
        out = None
        for t in range(tiles):
            term = picked[t] * take(scaled_ref[pl.ds(t * ROWS, ROWS), :], first)
            out = term if out is None else out + term
        out = out + pltpu.roll(out, pairs, 0)
        out_ref[q] = out[:pairs]

    def three(step, carry):
        places = [step * 3 + u for u in range(3)]
        ids = [block_of(q) for q in places]
        lane = jnp.concatenate([lane_ref[pl.ds(b, 1), :] for b in ids[:2]], axis=1)
        hot = jnp.where(inside == lane.astype(F32).astype(BF16), one, zero)
        offers = jnp.dot(basis_ref[...], jnp.concatenate([hot, hot], axis=0), preferred_element_type=F32)
        third_lane = row_of(lane_ref, ids[2])
        third = select(row_of(chunk_ref, ids[2]), lambda c, t: take(table_ref[c, pl.ds(t * ROWS, ROWS), :], third_lane))
        chunk = jnp.concatenate([row_of(chunk_ref, b) for b in ids[:2]], axis=1)
        picked = select(chunk, lambda c, t: offers[c * rows + t * ROWS : c * rows + (t + 1) * ROWS])
        for u in range(2):
            finish(places[u], ids[u], [value[:, u * LANES : (u + 1) * LANES] for value in picked])
        finish(places[2], ids[2], third)
        return carry

    lax.fori_loop(0, count // 3, three, 0, unroll=4)


def sweep_kernel(
    sizes,
    bands_ref,
    valence_energy_ref,
    conduction_energy_ref,
    frequency_ref,
    *refs,
):
    given, (out_ref, *kept), held = refs[:7], refs[7:10], refs[10:17]
    table_ref, scaled_ref, density_ref, fold_ref, *picking, sems, store_sems = refs[17:]
    stores = [pltpu.make_async_copy(source, target, store_sems.at[i]) for i, (source, target) in enumerate(zip((table_ref, scaled_ref), kept))]
    loads = [pltpu.make_async_copy(source, target, sems.at[i]) for i, (source, target) in enumerate(zip(given, held))]
    for load in loads:
        load.start()
    valence_ref, conduction_ref, z_high_ref, z_low_ref, y_ref, x_ref, index_ref = held
    extent, planes, pairs, total_pairs, count, block_of = sizes
    rows = planes * pairs
    tiles = rows // ROWS
    per_tile = ROWS // pairs
    per_chunk = 3 * LANES // extent
    groups = extent // per_chunk
    row_id = lax.broadcasted_iota(jnp.int32, (ROWS, LANES), 0)
    lane_id = lax.broadcasted_iota(jnp.int32, (ROWS, LANES), 1)
    band = jnp.zeros((ROWS, LANES), jnp.int32)
    for p in range(pairs):
        band = jnp.where(row_id % pairs == p, bands_ref[0, p], band)
    loads[0].wait()
    loads[1].wait()
    for m in range(groups):
        for part in range(3):
            lanes = pl.ds((m * 3 + part) * LANES, LANES)
            for t in range(tiles):
                value, factor = None, None
                for u in range(per_tile):
                    plane = t * per_tile + u
                    picked = jnp.take_along_axis(valence_ref[plane, :, lanes], band, axis=0, mode="promise_in_bounds")
                    other = jnp.broadcast_to(conduction_ref[plane, :, lanes], (ROWS, LANES))
                    value = picked if u == 0 else jnp.where(row_id >= u * pairs, picked, value)
                    factor = other if u == 0 else jnp.where(row_id >= u * pairs, other, factor)
                density_ref[part, pl.ds(m * rows + t * ROWS, ROWS), :] = value * factor
    density = jnp.concatenate([density_ref[part] for part in range(3)], axis=1)
    high, low = split(density)
    loads[2].wait()
    loads[3].wait()
    dot = functools.partial(jnp.dot, preferred_element_type=F32)
    swept = dot(high, z_high_ref[...]) + dot(low, z_high_ref[...]) + dot(high, z_low_ref[...])
    quarter = per_chunk // 2
    for m in range(groups // 2):
        for q in range(quarter):
            near = swept[m * rows : (m + 1) * rows, q * LANES : (q + 1) * LANES]
            far_m, far_q = groups - 1 - m, quarter - 1 - q
            far = swept[far_m * rows : (far_m + 1) * rows, far_q * LANES : (far_q + 1) * LANES]
            far = pltpu.roll(far, LANES // 2, 1)
            fold_ref[0, m * quarter + q] = near + far
            fold_ref[1, m * quarter + q] = near - far
    terms = extent // 4
    block = 2 * ROWS
    loads[4].wait()

    def sweep_tiles(t, carry):
        where_rows = pl.ds(pl.multiple_of(t * block, block), block)
        for parity in range(2):
            parts = [fold_ref[parity, s, where_rows, :] for s in range(terms)]
            for j in range(parity, extent, 2):
                total = None
                for s in range(terms):
                    term = parts[s] * y_ref[pl.ds(j * terms + s, 1), :]
                    total = term if total is None else total + term
                total = total + pltpu.roll(total, LANES // 2, 1)
                start = j * extent
                offset = start % LANES
                moved = total if offset % (LANES // 2) == 0 else pltpu.roll(total, offset, 1)
                for chunk in range(start // LANES, (start + extent - 1) // LANES + 1):
                    low_lane = max(start - chunk * LANES, 0)
                    high_lane = min(start + extent - chunk * LANES, LANES)
                    table_ref[chunk, where_rows, low_lane:high_lane] = moved[:, low_lane:high_lane]
        return carry

    lax.fori_loop(0, rows // block, sweep_tiles, 0)
    loads[5].wait()
    loads[6].wait()
    narrow_pos = lax.axis_index("narrow")
    gap = jnp.zeros((ROWS, LANES), F32)
    for p in range(pairs):
        one_gap = conduction_energy_ref[bands_ref[1, p]] - valence_energy_ref[bands_ref[0, p]]
        gap = jnp.where(row_id % pairs == p, one_gap, gap)
    frequency = frequency_ref[0]
    scale = jnp.sqrt(4.0 * gap / (gap * gap + frequency * frequency) / math.sqrt(total_pairs))
    for t in range(tiles):
        scaled_ref[pl.ds(t * ROWS, ROWS), :] = x_ref[narrow_pos, pl.ds(t * ROWS, ROWS), :] * scale
    for store in stores:
        store.start()
    pick_blocks(pairs, count, block_of(), index_ref, table_ref, scaled_ref, out_ref, *picking)
    for store in stores:
        store.wait()


def pick_kernel(pairs, count, block_of, *refs):
    given, out_ref, held, picking, sems = refs[:3], refs[3], refs[4:7], refs[7:11], refs[11]
    loads = [pltpu.make_async_copy(source, target, sems.at[i]) for i, (source, target) in enumerate(zip(given, held))]
    for load in loads:
        load.start()
    for load in loads:
        load.wait()
    pick_blocks(pairs, count, block_of(), *held, out_ref, *picking)


def pick_scratch(index, table):
    blocks, (chunks, rows, _) = index.shape[0], table.shape
    return [pltpu.VMEM((chunks * rows, 2 * LANES), BF16)] + [pltpu.VMEM((blocks, LANES), jnp.int32)] * 3


SMEM = pl.BlockSpec(memory_space=pltpu.SMEM)
VMEM = pl.BlockSpec(memory_space=pltpu.VMEM)
HBM = pl.BlockSpec(memory_space=pltpu.HBM)


def sweep_call(bands, valence_energy, conduction_energy, frequency, valence, conduction, index, total_pairs, count, block_of):
    pairs = bands.shape[1]
    planes, area = valence.shape[0], valence.shape[2]
    extent = math.isqrt(area)
    rows = planes * pairs
    cosine = cosine_table(extent)
    per_chunk = 3 * LANES // extent
    groups = extent // per_chunk
    weights = z_weights(cosine, per_chunk, LANES // 2)
    z_high = weights.astype(BF16)
    z_low = (weights - z_high.astype(np.float32)).astype(BF16)
    operands = [valence, conduction, jnp.asarray(z_high), jnp.asarray(z_low)]
    operands += [jnp.asarray(y_weights(cosine)), jnp.asarray(x_tables(cosine, planes, pairs)), index]
    chunks = area // LANES
    table = jax.ShapeDtypeStruct((area // LANES, rows, LANES), F32)
    scaled = jax.ShapeDtypeStruct((rows, LANES), F32)
    return pl.pallas_call(
        functools.partial(sweep_kernel, (extent, planes, pairs, total_pairs, count, block_of)),
        out_shape=[jax.ShapeDtypeStruct((count, pairs, LANES), F32), table, scaled],
        in_specs=[SMEM] * 4 + [HBM] * len(operands),
        out_specs=[VMEM, HBM, HBM],
        scratch_shapes=[pltpu.VMEM(a.shape, a.dtype) for a in operands]
        + [
            pltpu.VMEM(table.shape, F32),
            pltpu.VMEM(scaled.shape, F32),
            pltpu.VMEM((3, groups * rows, LANES), F32),
            pltpu.VMEM((2, extent // 4, rows, LANES), F32),
        ]
        + pick_scratch(index, table)
        + [pltpu.SemaphoreType.DMA((len(operands),)), pltpu.SemaphoreType.DMA((2,))],
        cost_estimate=pl.CostEstimate(flops=8_000_000_000, bytes_accessed=4_000_000, transcendentals=0),
        name="sweep",
    )(bands, valence_energy, conduction_energy, frequency, *operands)


def pick_call(index, table, scaled, pairs, count, block_of):
    operands = (index, table, scaled)
    return pl.pallas_call(
        functools.partial(pick_kernel, pairs, count, block_of),
        out_shape=jax.ShapeDtypeStruct((count, pairs, LANES), F32),
        in_specs=[HBM] * 3,
        out_specs=VMEM,
        scratch_shapes=[pltpu.VMEM(a.shape, a.dtype) for a in operands] + pick_scratch(index, table) + [pltpu.SemaphoreType.DMA((3,))],
        cost_estimate=pl.CostEstimate(flops=4_000_000_000, bytes_accessed=1_000_000, transcendentals=0),
        name="pick",
    )(*operands)


def arrange_kernel(row_tiles, near_ref, far_ref, own_ref, wide_ref, narrow_ref, both_ref):
    narrow_count = lax.axis_size("narrow")
    half = narrow_count * row_tiles
    wide_pos, narrow_pos = lax.axis_index("wide"), lax.axis_index("narrow")
    for out_ref, w, n in (
        (own_ref, wide_pos, narrow_pos),
        (wide_ref, 1 - wide_pos, narrow_pos),
        (narrow_ref, wide_pos, narrow_pos ^ 1),
        (both_ref, 1 - wide_pos, narrow_pos ^ 1),
    ):
        columns = pl.ds(w * half, half)
        rows = pl.ds((1 - w) * half + n * row_tiles, row_tiles)
        out_ref[pl.ds(0, half)] = near_ref[columns] + far_ref[columns]
        out_ref[pl.ds(half, row_tiles)] = near_ref[rows] + far_ref[rows]


def arrange_call(near, far, row_tiles):
    blocks, pairs, _ = near.shape
    shape = (blocks // 2 + row_tiles, pairs, LANES)
    return pl.pallas_call(
        functools.partial(arrange_kernel, row_tiles),
        out_shape=[jax.ShapeDtypeStruct(shape, F32)] * 4,
        in_specs=[VMEM] * 2,
        out_specs=[VMEM] * 4,
        compiler_params=pltpu.CompilerParams(vmem_limit_bytes=16 << 20),
        name="arrange",
    )(near, far)


def product_kernel(row_tiles, pairs, own_ref, across_ref, core_ref, far_ref, out_ref, rows_ref, gather_ref, value_ref, sems):
    section, wide_pos, narrow_pos = lax.axis_index("section"), lax.axis_index("wide"), lax.axis_index("narrow")
    parity = narrow_pos & 1
    narrow_count = lax.axis_size("narrow")
    half = narrow_count * row_tiles
    sources = (own_ref, across_ref, core_ref, far_ref)
    row_block = rows_ref.shape[0]

    def collect(kind, start):
        for i, ref in enumerate(sources):
            for b in range(2):
                rows = pl.ds((2 * i + b) * pairs, pairs)
                for r in range(row_tiles):
                    gather_ref[rows, pl.ds(r * LANES, LANES)] = ref[2 * kind + b, start + r]
        return gather_ref[...]

    start = jnp.where(section // 2 == wide_pos, narrow_pos * row_tiles, half)
    high, low = split(-collect((section & 1) ^ parity, start))
    high, low = high.astype(F32), low.astype(F32)
    rows_ref[...] = jnp.concatenate([high, high, low, low], axis=0).T.astype(BF16)

    def copy_of(step):
        columns = pl.ds(pl.multiple_of(step * row_block, row_block), row_block)
        return pltpu.make_async_copy(value_ref.at[:, columns], out_ref.at[:, columns], sems.at[step])

    def one_block(step, carry):
        high, low = split(collect((step // narrow_count) ^ parity, (step % narrow_count) * row_tiles))
        stacked = jnp.concatenate([high, low, high, low], axis=0)
        columns = pl.ds(pl.multiple_of(step * row_block, row_block), row_block)
        value_ref[:, columns] = jnp.dot(rows_ref[...], stacked, preferred_element_type=F32)
        copy_of(step).start()
        return carry

    def wait_block(step, carry):
        copy_of(step).wait()
        return carry

    steps = 2 * narrow_count
    lax.fori_loop(0, steps, one_block, 0)
    lax.fori_loop(0, steps, wait_block, 0)


def product_call(sources, row_tiles):
    _, blocks, pairs, _ = sources[0].shape
    row_block = row_tiles * LANES
    steps = 2 * (blocks // row_tiles - 1)
    depth = 2 * len(sources) * pairs
    return pl.pallas_call(
        functools.partial(product_kernel, row_tiles, pairs),
        out_shape=jax.ShapeDtypeStruct((row_block, steps * row_block), F32),
        in_specs=[VMEM] * len(sources),
        out_specs=pl.BlockSpec(memory_space=pl.ANY),
        scratch_shapes=[
            pltpu.VMEM((row_block, 4 * depth), BF16),
            pltpu.VMEM((depth, row_block), F32),
            pltpu.VMEM((row_block, steps * row_block), F32),
            pltpu.SemaphoreType.DMA((steps,)),
        ],
        compiler_params=pltpu.CompilerParams(vmem_limit_bytes=40 << 20),
        name="product",
    )(*sources)


def contract(left_rows, right_rows):
    return lax.dot_general(
        left_rows,
        right_rows,
        (((0,), (0,)), ((), ())),
        precision=lax.Precision.HIGHEST,
        preferred_element_type=F32,
    )


def on_device(valence, conduction, valence_energy, conduction_energy, frequency, pair_bands, gvec_index):
    pairs = pair_bands.shape[0]
    section_count, wide_count, narrow_count = (lax.axis_size(name) for name in ("section", "wide", "narrow"))
    total_pairs = pairs * section_count * wide_count
    vector_count = gvec_index.shape[0]
    row_block = vector_count // (section_count * narrow_count)
    column_block = vector_count // wide_count
    row_tiles = row_block // LANES
    blocks = vector_count // LANES
    index = gvec_index.reshape(blocks, LANES)
    valence, conduction = (jnp.swapaxes(orbitals, 0, 1) for orbitals in (valence, conduction))
    energies = (valence_energy, conduction_energy, frequency)
    sweep = functools.partial(sweep_call, pair_bands.T, *energies, valence, conduction, index, total_pairs)

    if not (section_count == 4 and wide_count == 2 and narrow_count == 4):
        partial_value = sweep(blocks, lambda: lambda q: q)[0]
        partial_value = jnp.swapaxes(partial_value, 0, 1).reshape(pairs, section_count, narrow_count, row_block)
        own_rows = lax.psum_scatter(partial_value, "narrow", scatter_dimension=2, tiled=True)
        coefficients = lax.all_gather(own_rows, "narrow", axis=2, tiled=True).reshape(pairs, vector_count)
        row_send = own_rows.reshape(pairs, section_count, row_block)
        row_recv = lax.all_to_all(row_send, "section", split_axis=1, concat_axis=0, tiled=True)
        row_recv = row_recv.reshape(section_count, pairs, row_block)
        column_send = coefficients.reshape(pairs, wide_count, column_block)
        column_recv = lax.all_to_all(column_send, "wide", split_axis=1, concat_axis=0, tiled=True)
        column_recv = column_recv.reshape(wide_count * pairs, column_block)
        rows_all = lax.all_gather(row_recv, "wide", axis=1, tiled=True).reshape(-1, row_block)
        return contract(-rows_all, lax.all_gather(column_recv, "section", axis=0, tiled=True))

    half = narrow_count * row_tiles

    def block_of(other):
        def make():
            own = (lax.axis_index("narrow") & 1) ^ other
            return lambda q: q + (q // half + own) * half

        return make

    away, table, scaled = sweep(blocks // 2, block_of(1))
    kept = pick_call(index, table, scaled, pairs, blocks // 2, block_of(0))
    flip = lambda bit: [(i, i ^ bit) for i in range(4)]
    summed = kept + lax.ppermute(away, "narrow", flip(1))
    opposite = lax.ppermute(summed, "narrow", flip(2))
    own, to_wide, to_narrow, to_both = arrange_call(summed, opposite, row_tiles)
    from_wide = lax.ppermute(to_wide, "wide", [(0, 1), (1, 0)])
    from_narrow = lax.ppermute(to_narrow, "narrow", flip(1))
    from_both = lax.ppermute(to_both, ("wide", "narrow"), [(i, i ^ 5) for i in range(8)])
    near = jnp.stack([own, from_wide, from_narrow, from_both])
    across = lax.ppermute(near, "section", flip(2))
    core = lax.ppermute(near, "section", flip(1))
    far = lax.ppermute(across, "section", flip(1))
    return product_call((near, across, core, far), row_tiles)


def solution(mesh):
    in_specs = (
        P(None, "narrow", None),
        P(("section", "wide"), "narrow", None),
        P(),
        P(),
        P(),
        P(("section", "wide"), None),
        P(),
    )
    out_specs = P(("section", "narrow"), "wide")
    return jax.shard_map(on_device, mesh=mesh, in_specs=in_specs, out_specs=out_specs, check_vma=False)
```

time: 59.5 us -> 47.7 us (0.80)
  local copies, waits for them, and re-layouts: 6.71 us -> 0 us
  Pallas kernels: 24.9 us -> 20.8 us
  other arithmetic: 1.81 us -> 0.98 us
    unnamed x15 -> x0, local copies, waits for them, and re-layouts: 6.71 us -> none
    pallas_call x3, Pallas kernels: 16.5 us -> 11.9 us  [the longest x1 7.2 us: product_call(): pl.pallas_call(functools.partial(product_kernel, row_tiles, pairs), out_s...]
    another operation x1, other arithmetic: 0.89 us -> 0.06 us  [on_device(): near = jnp.stack([own, from_wide, from_narrow, from_both])]
  transfers between devices with their start and end apart: 8 -> 8, of which waited for: 6 -> 6; matrix products, arithmetic and copies ran while one was open for 0% -> 0% of each run, Pallas kernels for 9% -> 10%
where the time goes in v2:
time: 47.7 us; the launch traced here: 47.5 us
  Pallas kernels  20.8 us (44%)
  waiting for transfers between devices  14.1 us (30%)
  starting transfers between devices  10.9 us (23%)
  other arithmetic  0.98 us (2%)
  between operations  0.69 us (1%)
    pallas_call x1, Pallas kernels, sweep_call(): pl.pallas_call(functools.partial(sweep_kernel, (extent, planes, pairs, to...  8.89 us
    pallas_call x1, Pallas kernels, product_call(): pl.pallas_call(functools.partial(product_kernel, row_tiles, pairs), out_s...  7.2 us
    ppermute x1, waiting for transfers between devices, on_device(): across = lax.ppermute(near, 'section', flip(2))  4.87 us
    pallas_call x1, Pallas kernels, pick_call(): pl.pallas_call(functools.partial(pick_kernel, pairs, count, block_of), ou...  4.66 us
    ppermute x1, waiting for transfers between devices, on_device(): opposite = lax.ppermute(summed, 'narrow', flip(2))  4.51 us
    ppermute x1, starting transfers between devices, on_device(): summed = kept + lax.ppermute(away, 'narrow', flip(1))  3.12 us
    ppermute x1, starting transfers between devices, on_device(): opposite = lax.ppermute(summed, 'narrow', flip(2))  2.65 us
    ppermute x1, starting transfers between devices, on_device(): lax.ppermute(to_both, ('wide', 'narrow'), [(i, i ^ 5) for i in range(8)])  1.91 us
  transfers between devices with their start and end apart: 8, of which 6 were waited for; matrix products, arithmetic and copies ran while one was open for 0% of the time, Pallas kernels for 10%

profile of v2, /device:TPU:0, one launch (start us, length us, event | category | flops | bytes accessed | tf_op | source)
XLA Modules:
  0.0 47.5 jit_solution(10420354701774528762)
XLA Ops:
  0.7 8.9 %sweep.1 = (f32[48,4,128]{2,1,0:T(4,128)}, f32[18,48,128]{2,1,0:T(8,128)}, f32[48,128]{1,0:T(8,128)}) custom-call(s32[2,4]{1,0:T(2,128)} %bitcast.16, f32[8]{0:T(128)} %valence_energy_ref.1, f32[8]{0:T(128)} %conduction_energy_ref.1, f32[1]{0:T(128)S(6)} %copy.12.frequency_ref, f32[12,8,2304]{2,1,0:T(8,128)} %bitcast.12, f32[12,1,2304]{2,1,0:T(1,128)} %bitcast.13, ...), custom_call_target="tpu_custom_call" | custom-call | flops 8000000000 | bytes 4000000 | tf_op jit(solution)/shard_map/sweep/pallas_call | solution.py:248
  9.6 3.1 %collective-permute-start = (f32[48,4,128]{2,1,0:T(4,128)}, f32[48,4,128]{2,1,0:T(4,128)S(1)}, u32[]{:S(2)}, u32[]{:S(2)}) collective-permute-start(f32[48,4,128]{2,1,0:T(4,128)} %get-tuple-element.14), channel_id=1, source_target_pairs={{0,1},{1,0},{2,3},{3,2},{4,5},{5,4},{6,7},{7,6},{8,9},{9,8},{10,11... | collective-permute-start | bytes 294920 | tf_op jit(solution)/shard_map/ppermute | solution.py:422
  12.7 4.7 %pick.1 = f32[48,4,128]{2,1,0:T(4,128)} custom-call(s32[96,128]{1,0:T(8,128)} %bitcast.15, f32[18,48,128]{2,1,0:T(8,128)} %get-tuple-element.12.refs_1_, f32[48,128]{1,0:T(8,128)} %get-tuple-element.13.refs_2_), custom_call_target="tpu_custom_call" | custom-call | flops 4000000000 | bytes 1000000 | tf_op jit(solution)/shard_map/pick/pallas_call | solution.py:269
  17.3 0.0 collective-permute-done
  17.3 0.9 %add.3.near_ref = f32[48,4,128]{2,1,0:T(4,128)S(1)} add(f32[48,4,128]{2,1,0:T(4,128)} %pick.1, f32[48,4,128]{2,1,0:T(4,128)S(1)} %collective-permute-done) | non-fusion elementwise | flops 24576 | bytes 294912 | tf_op jit(solution)/shard_map/add | solution.py:422
  18.3 2.7 %collective-permute-start.1 = (f32[48,4,128]{2,1,0:T(4,128)S(1)}, f32[48,4,128]{2,1,0:T(4,128)S(1)}, u32[]{:S(2)}, u32[]{:S(2)}) collective-permute-start(f32[48,4,128]{2,1,0:T(4,128)S(1)} %add.3.near_ref), channel_id=1, source_target_pairs={{0,2},{1,3},{2,0},{3,1},{4,6},{5,7},{6,4},{7,5},{8,10},{9,11},{10,... | collective-permute-start | bytes 294920 | tf_op jit(solution)/shard_map/ppermute | solution.py:423
  20.9 4.5 %collective-permute-done.1.far_ref = f32[48,4,128]{2,1,0:T(4,128)S(1)} collective-permute-done((f32[48,4,128]{2,1,0:T(4,128)S(1)}, f32[48,4,128]{2,1,0:T(4,128)S(1)}, u32[]{:S(2)}, u32[]{:S(2)}) %collective-permute-start.1) | collective-permute-done | bytes 98336 | tf_op jit(solution)/shard_map/ppermute | solution.py:423
  25.5 1.6 %collective-permute-start.2 = (f32[30,4,128]{2,1,0:T(4,128)S(1)}, f32[30,4,128]{2,1,0:T(4,128)S(1)}, u32[]{:S(2)}, u32[]{:S(2)}) collective-permute-start(f32[30,4,128]{2,1,0:T(4,128)S(1)} %get-tuple-element.16), channel_id=1, source_target_pairs={{0,4},{4,0},{1,5},{5,1},{2,6},{6,2},{3,7},{7,3},{8,12},{12,8},{9,1... | collective-permute-start | bytes 184328 | tf_op jit(solution)/shard_map/ppermute | solution.py:425
  27.1 0.0 collective-permute-start.3
  27.1 1.9 %collective-permute-start.4 = (f32[30,4,128]{2,1,0:T(4,128)S(1)}, f32[30,4,128]{2,1,0:T(4,128)S(1)}, u32[]{:S(2)}, u32[]{:S(2)}) collective-permute-start(f32[30,4,128]{2,1,0:T(4,128)S(1)} %get-tuple-element.18), channel_id=1, source_target_pairs={{0,5},{1,4},{2,7},{3,6},{4,1},{5,0},{6,3},{7,2},{8,13},{9,12},{10,... | collective-permute-start | bytes 184328 | tf_op jit(solution)/shard_map/ppermute | solution.py:427
  29.0 0.7 %collective-permute-done.2 = f32[30,4,128]{2,1,0:T(4,128)S(1)} collective-permute-done((f32[30,4,128]{2,1,0:T(4,128)S(1)}, f32[30,4,128]{2,1,0:T(4,128)S(1)}, u32[]{:S(2)}, u32[]{:S(2)}) %collective-permute-start.2) | collective-permute-done | bytes 61472 | tf_op jit(solution)/shard_map/ppermute | solution.py:425
  29.8 1.6 %collective-permute-done.3 = f32[30,4,128]{2,1,0:T(4,128)S(1)} collective-permute-done((f32[30,4,128]{2,1,0:T(4,128)S(1)}, f32[30,4,128]{2,1,0:T(4,128)S(1)}, u32[]{:S(2)}, u32[]{:S(2)}) %collective-permute-start.3) | collective-permute-done | bytes 61472 | tf_op jit(solution)/shard_map/ppermute | solution.py:426
  31.4 0.9 %collective-permute-done.4 = f32[30,4,128]{2,1,0:T(4,128)S(1)} collective-permute-done((f32[30,4,128]{2,1,0:T(4,128)S(1)}, f32[30,4,128]{2,1,0:T(4,128)S(1)}, u32[]{:S(2)}, u32[]{:S(2)}) %collective-permute-start.4) | collective-permute-done | bytes 61472 | tf_op jit(solution)/shard_map/ppermute | solution.py:427
  32.3 0.1 pad_maximum_fusion.own_ref
  32.3 1.6 %collective-permute-start.5 = (f32[4,30,4,128]{3,2,1,0:T(4,128)S(1)}, f32[4,30,4,128]{3,2,1,0:T(4,128)S(1)}, u32[]{:S(2)}, u32[]{:S(2)}) collective-permute-start(f32[4,30,4,128]{3,2,1,0:T(4,128)S(1)} %pad_maximum_fusion.own_ref), channel_id=1, source_target_pairs={{0,16},{8,24},{16,0},{24,8},{1,17},{9,25},{17,1},{25,9},{2,18},{10... | collective-permute-start | bytes 737288 | tf_op jit(solution)/shard_map/ppermute | solution.py:429
  33.9 0.0 collective-permute-start.6
  33.9 4.9 %collective-permute-done.5.across_ref = f32[4,30,4,128]{3,2,1,0:T(4,128)S(1)} collective-permute-done((f32[4,30,4,128]{3,2,1,0:T(4,128)S(1)}, f32[4,30,4,128]{3,2,1,0:T(4,128)S(1)}, u32[]{:S(2)}, u32[]{:S(2)}) %collective-permute-start.5) | collective-permute-done | bytes 245792 | tf_op jit(solution)/shard_map/ppermute | solution.py:429
  38.7 0.0 collective-permute-start.7
  38.7 0.0 collective-permute-done.6.core_ref
  38.7 1.5 %collective-permute-done.7.far_ref = f32[4,30,4,128]{3,2,1,0:T(4,128)S(1)} collective-permute-done((f32[4,30,4,128]{3,2,1,0:T(4,128)S(1)}, f32[4,30,4,128]{3,2,1,0:T(4,128)S(1)}, u32[]{:S(2)}, u32[]{:S(2)}) %collective-permute-start.7) | collective-permute-done | bytes 245792 | tf_op jit(solution)/shard_map/ppermute | solution.py:431
  40.3 7.2 %product.1 = f32[768,6144]{1,0:T(8,128)} custom-call(f32[4,30,4,128]{3,2,1,0:T(4,128)S(1)} %pad_maximum_fusion.own_ref, f32[4,30,4,128]{3,2,1,0:T(4,128)S(1)} %collective-permute-done.5.across_ref, f32[4,30,4,128]{3,2,1,0:T(4,128)S(1)} %collective-permute-done.6.core_ref, f32[4,30,4,128]{3,2,1,0:T(4,128)S(1)} %collective-permute-done.7.far_ref), custom_call_target="tpu_custom_call" | custom-call | tf_op jit(solution)/shard_map/product/pallas_call | solution.py:356
  (1 shorter events, 0.0 us)
Async XLA Ops:
  9.6 7.8 %collective-permute-start = (f32[48,4,128]{2,1,0:T(4,128)}, f32[48,4,128]{2,1,0:T(4,128)S(1)}, u32[]{:S(2)}, u32[]{:S(2)}) collective-permute-start(f32[48,4,128]{2,1,0:T(4,128)} %get-tuple-element.14), channel_id=1, source_target_pairs={{0,1},{1,0},{2,3},{3,2},{4,5},{5,4},{6,7},{7,6},{8,9},{9,8},{10,11... | collective-permute-start | bytes 294920 | tf_op jit(solution)/shard_map/ppermute | solution.py:422
  18.3 7.2 %collective-permute-start.1 = (f32[48,4,128]{2,1,0:T(4,128)S(1)}, f32[48,4,128]{2,1,0:T(4,128)S(1)}, u32[]{:S(2)}, u32[]{:S(2)}) collective-permute-start(f32[48,4,128]{2,1,0:T(4,128)S(1)} %add.3.near_ref), channel_id=1, source_target_pairs={{0,2},{1,3},{2,0},{3,1},{4,6},{5,7},{6,4},{7,5},{8,10},{9,11},{10,... | collective-permute-start | bytes 294920 | tf_op jit(solution)/shard_map/ppermute | solution.py:423
  25.5 4.3 %collective-permute-start.2 = (f32[30,4,128]{2,1,0:T(4,128)S(1)}, f32[30,4,128]{2,1,0:T(4,128)S(1)}, u32[]{:S(2)}, u32[]{:S(2)}) collective-permute-start(f32[30,4,128]{2,1,0:T(4,128)S(1)} %get-tuple-element.16), channel_id=1, source_target_pairs={{0,4},{4,0},{1,5},{5,1},{2,6},{6,2},{3,7},{7,3},{8,12},{12,8},{9,1... | collective-permute-start | bytes 184328 | tf_op jit(solution)/shard_map/ppermute | solution.py:425
  27.1 4.2 %collective-permute-start.3 = (f32[30,4,128]{2,1,0:T(4,128)S(1)}, f32[30,4,128]{2,1,0:T(4,128)S(1)}, u32[]{:S(2)}, u32[]{:S(2)}) collective-permute-start(f32[30,4,128]{2,1,0:T(4,128)S(1)} %get-tuple-element.17), channel_id=1, source_target_pairs={{0,1},{1,0},{2,3},{3,2},{4,5},{5,4},{6,7},{7,6},{8,9},{9,8},{10,11... | collective-permute-start | bytes 184328 | tf_op jit(solution)/shard_map/ppermute | solution.py:426
  27.1 5.1 %collective-permute-start.4 = (f32[30,4,128]{2,1,0:T(4,128)S(1)}, f32[30,4,128]{2,1,0:T(4,128)S(1)}, u32[]{:S(2)}, u32[]{:S(2)}) collective-permute-start(f32[30,4,128]{2,1,0:T(4,128)S(1)} %get-tuple-element.18), channel_id=1, source_target_pairs={{0,5},{1,4},{2,7},{3,6},{4,1},{5,0},{6,3},{7,2},{8,13},{9,12},{10,... | collective-permute-start | bytes 184328 | tf_op jit(solution)/shard_map/ppermute | solution.py:427
  32.3 6.4 %collective-permute-start.5 = (f32[4,30,4,128]{3,2,1,0:T(4,128)S(1)}, f32[4,30,4,128]{3,2,1,0:T(4,128)S(1)}, u32[]{:S(2)}, u32[]{:S(2)}) collective-permute-start(f32[4,30,4,128]{3,2,1,0:T(4,128)S(1)} %pad_maximum_fusion.own_ref), channel_id=1, source_target_pairs={{0,16},{8,24},{16,0},{24,8},{1,17},{9,25},{17,1},{25,9},{2,18},{10... | collective-permute-start | bytes 737288 | tf_op jit(solution)/shard_map/ppermute | solution.py:429
  33.9 4.9 %collective-permute-start.6 = (f32[4,30,4,128]{3,2,1,0:T(4,128)S(1)}, f32[4,30,4,128]{3,2,1,0:T(4,128)S(1)}, u32[]{:S(2)}, u32[]{:S(2)}) collective-permute-start(f32[4,30,4,128]{3,2,1,0:T(4,128)S(1)} %pad_maximum_fusion.own_ref), channel_id=1, source_target_pairs={{0,8},{8,0},{16,24},{24,16},{1,9},{9,1},{17,25},{25,17},{2,10},{10... | collective-permute-start | bytes 737288 | tf_op jit(solution)/shard_map/ppermute | solution.py:430
  38.7 1.5 %collective-permute-start.7 = (f32[4,30,4,128]{3,2,1,0:T(4,128)S(1)}, f32[4,30,4,128]{3,2,1,0:T(4,128)S(1)}, u32[]{:S(2)}, u32[]{:S(2)}) collective-permute-start(f32[4,30,4,128]{3,2,1,0:T(4,128)S(1)} %collective-permute-done.5.across_ref), channel_id=1, source_target_pairs={{0,8},{8,0},{16,24},{24,16},{1,9},{9,1},{17,25},{25,17},{2,10},{10... | collective-permute-start | bytes 737288 | tf_op jit(solution)/shard_map/ppermute | solution.py:431

commit v3 on v2

--- a/solution.py
+++ b/solution.py
@@ -54,14 +54,16 @@
     return out
 
 
-def pick_blocks(pairs, count, block_of, index_ref, table_ref, scaled_ref, out_ref, basis_ref, lane_ref, chunk_ref, first_ref):
-    per_plane, rows, _ = table_ref.shape
+def pick_blocks(pairs, count, block_of, table_ref, out_ref, basis_ref, lane_ref, chunk_ref, first_ref):
+    rows = table_ref.shape[1]
+    per_plane = basis_ref.shape[0] // rows
     tiles = rows // ROWS
+    scaled_ref = table_ref.at[per_plane]
     for s in range(per_plane):
         high, low = split(table_ref[s])
         basis_ref[pl.ds(s * rows, rows), pl.ds(0, LANES)] = high
         basis_ref[pl.ds(s * rows, rows), pl.ds(LANES, LANES)] = low
-    index = index_ref[...]
+    index = table_ref[per_plane + 1 :].reshape(-1, LANES)[: lane_ref.shape[0]].astype(jnp.int32)
     lane_ref[...] = index & (LANES - 1)
     upper = index >> (LANES.bit_length() - 1)
     plane = (upper * ((1 << 16) // per_plane + 1)) >> 16
@@ -109,24 +111,24 @@
         finish(places[2], ids[2], third)
         return carry
 
-    lax.fori_loop(0, count // 3, three, 0, unroll=4)
+    lax.fori_loop(0, count // 3, three, 0, unroll=8)
 
 
 def sweep_kernel(
     sizes,
-    bands_ref,
-    valence_energy_ref,
-    conduction_energy_ref,
-    frequency_ref,
     *refs,
 ):
-    given, (out_ref, *kept), held = refs[:7], refs[7:10], refs[10:17]
-    table_ref, scaled_ref, density_ref, fold_ref, *picking, sems, store_sems = refs[17:]
-    stores = [pltpu.make_async_copy(source, target, store_sems.at[i]) for i, (source, target) in enumerate(zip((table_ref, scaled_ref), kept))]
+    given, (out_ref, kept_ref), held = refs[:11], refs[11:13], refs[13:24]
+    table_ref, density_ref, fold_ref, *picking, sems, store_sem = refs[24:]
+    store = pltpu.make_async_copy(table_ref, kept_ref, store_sem)
     loads = [pltpu.make_async_copy(source, target, sems.at[i]) for i, (source, target) in enumerate(zip(given, held))]
     for load in loads:
         load.start()
+    bands_ref, valence_energy_ref, conduction_energy_ref, frequency_ref, *held = held
     valence_ref, conduction_ref, z_high_ref, z_low_ref, y_ref, x_ref, index_ref = held
+    for load in loads[:4]:
+        load.wait()
+    loads = loads[4:]
     extent, planes, pairs, total_pairs, count, block_of = sizes
     rows = planes * pairs
     tiles = rows // ROWS
@@ -191,6 +193,7 @@
         return carry
 
     lax.fori_loop(0, rows // block, sweep_tiles, 0)
+    per_plane = extent * extent // LANES
     loads[5].wait()
     loads[6].wait()
     narrow_pos = lax.axis_index("narrow")
@@ -201,30 +204,24 @@
     frequency = frequency_ref[0]
     scale = jnp.sqrt(4.0 * gap / (gap * gap + frequency * frequency) / math.sqrt(total_pairs))
     for t in range(tiles):
-        scaled_ref[pl.ds(t * ROWS, ROWS), :] = x_ref[narrow_pos, pl.ds(t * ROWS, ROWS), :] * scale
-    for store in stores:
-        store.start()
-    pick_blocks(pairs, count, block_of(), index_ref, table_ref, scaled_ref, out_ref, *picking)
-    for store in stores:
-        store.wait()
+        table_ref[per_plane, pl.ds(t * ROWS, ROWS), :] = x_ref[narrow_pos, pl.ds(t * ROWS, ROWS), :] * scale
+    blocks = index_ref.shape[0]
+    for i in range(table_ref.shape[0] - per_plane - 1):
+        some = min(rows, blocks - i * rows)
+        table_ref[per_plane + 1 + i, pl.ds(0, some), :] = index_ref[pl.ds(i * rows, some), :].astype(F32)
+    store.start()
+    pick_blocks(pairs, count, block_of(), table_ref, out_ref, *picking)
+    store.wait()
 
 
 def pick_kernel(pairs, count, block_of, *refs):
-    given, out_ref, held, picking, sems = refs[:3], refs[3], refs[4:7], refs[7:11], refs[11]
-    loads = [pltpu.make_async_copy(source, target, sems.at[i]) for i, (source, target) in enumerate(zip(given, held))]
-    for load in loads:
-        load.start()
-    for load in loads:
-        load.wait()
-    pick_blocks(pairs, count, block_of(), *held, out_ref, *picking)
-
-
-def pick_scratch(index, table):
-    blocks, (chunks, rows, _) = index.shape[0], table.shape
-    return [pltpu.VMEM((chunks * rows, 2 * LANES), BF16)] + [pltpu.VMEM((blocks, LANES), jnp.int32)] * 3
-
-
-SMEM = pl.BlockSpec(memory_space=pltpu.SMEM)
+    pick_blocks(pairs, count, block_of(), *refs)
+
+
+def pick_scratch(blocks, rows, area):
+    return [pltpu.VMEM((area // LANES * rows, 2 * LANES), BF16)] + [pltpu.VMEM((blocks, LANES), jnp.int32)] * 3
+
+
 VMEM = pl.BlockSpec(memory_space=pltpu.VMEM)
 HBM = pl.BlockSpec(memory_space=pltpu.HBM)
 
@@ -243,38 +240,39 @@
     operands = [valence, conduction, jnp.asarray(z_high), jnp.asarray(z_low)]
     operands += [jnp.asarray(y_weights(cosine)), jnp.asarray(x_tables(cosine, planes, pairs)), index]
     chunks = area // LANES
-    table = jax.ShapeDtypeStruct((area // LANES, rows, LANES), F32)
-    scaled = jax.ShapeDtypeStruct((rows, LANES), F32)
+    blocks = index.shape[0]
+    table = jax.ShapeDtypeStruct((area // LANES + 1 + -(-blocks // rows), rows, LANES), F32)
+    scalars = [bands, valence_energy, conduction_energy, frequency]
     return pl.pallas_call(
         functools.partial(sweep_kernel, (extent, planes, pairs, total_pairs, count, block_of)),
-        out_shape=[jax.ShapeDtypeStruct((count, pairs, LANES), F32), table, scaled],
-        in_specs=[SMEM] * 4 + [HBM] * len(operands),
-        out_specs=[VMEM, HBM, HBM],
-        scratch_shapes=[pltpu.VMEM(a.shape, a.dtype) for a in operands]
+        out_shape=[jax.ShapeDtypeStruct((count, pairs, LANES), F32), table],
+        in_specs=[HBM] * (len(scalars) + len(operands)),
+        out_specs=[VMEM, HBM],
+        scratch_shapes=[pltpu.SMEM(a.shape, a.dtype) for a in scalars]
+        + [pltpu.VMEM(a.shape, a.dtype) for a in operands]
         + [
             pltpu.VMEM(table.shape, F32),
-            pltpu.VMEM(scaled.shape, F32),
             pltpu.VMEM((3, groups * rows, LANES), F32),
             pltpu.VMEM((2, extent // 4, rows, LANES), F32),
         ]
-        + pick_scratch(index, table)
-        + [pltpu.SemaphoreType.DMA((len(operands),)), pltpu.SemaphoreType.DMA((2,))],
+        + pick_scratch(blocks, rows, area)
+        + [pltpu.SemaphoreType.DMA((len(scalars) + len(operands),)), pltpu.SemaphoreType.DMA],
         cost_estimate=pl.CostEstimate(flops=8_000_000_000, bytes_accessed=4_000_000, transcendentals=0),
         name="sweep",
-    )(bands, valence_energy, conduction_energy, frequency, *operands)
-
-
-def pick_call(index, table, scaled, pairs, count, block_of):
-    operands = (index, table, scaled)
+    )(*scalars, *operands)
+
+
+def pick_call(table, blocks, area, pairs, count, block_of):
     return pl.pallas_call(
         functools.partial(pick_kernel, pairs, count, block_of),
         out_shape=jax.ShapeDtypeStruct((count, pairs, LANES), F32),
-        in_specs=[HBM] * 3,
+        in_specs=[VMEM],
         out_specs=VMEM,
-        scratch_shapes=[pltpu.VMEM(a.shape, a.dtype) for a in operands] + pick_scratch(index, table) + [pltpu.SemaphoreType.DMA((3,))],
+        scratch_shapes=pick_scratch(blocks, table.shape[1], area),
+        compiler_params=pltpu.CompilerParams(vmem_limit_bytes=32 << 20),
         cost_estimate=pl.CostEstimate(flops=4_000_000_000, bytes_accessed=1_000_000, transcendentals=0),
         name="pick",
-    )(*operands)
+    )(table)
 
 
 def arrange_kernel(row_tiles, near_ref, far_ref, own_ref, wide_ref, narrow_ref, both_ref):
@@ -416,8 +414,8 @@
 
         return make
 
-    away, table, scaled = sweep(blocks // 2, block_of(1))
-    kept = pick_call(index, table, scaled, pairs, blocks // 2, block_of(0))
+    away, table = sweep(blocks // 2, block_of(1))
+    kept = pick_call(table, blocks, valence.shape[2], pairs, blocks // 2, block_of(0))
     flip = lambda bit: [(i, i ^ bit) for i in range(4)]
     summed = kept + lax.ppermute(away, "narrow", flip(1))
     opposite = lax.ppermute(summed, "narrow", flip(2))

time: 47.7 us -> 44.8 us (0.939)
  Pallas kernels: 20.8 us -> 18 us
  local copies, waits for them, and re-layouts: 0 us -> 1.04 us
  other arithmetic: 0.98 us -> 0.09 us
    pallas_call x1, Pallas kernels: 4.66 us -> 2.74 us  [pick_call(): pl.pallas_call(functools.partial(pick_kernel, pairs, count, block_of), ou...]
    unnamed x0 -> x2, local copies, waits for them, and re-layouts: none -> 1.04 us
    add x1, other arithmetic: 0.92 us -> 0.03 us  [on_device(): summed = kept + lax.ppermute(away, 'narrow', flip(1))]
    pallas_call x1, Pallas kernels: 8.89 us -> 8.02 us  [sweep_call(): pl.pallas_call(functools.partial(sweep_kernel, (extent, planes, pairs, to...]
  transfers between devices with their start and end apart: 8 -> 8, of which waited for: 6 -> 6; matrix products, arithmetic and copies ran while one was open for 0% -> 0% of each run, Pallas kernels for 10% -> 6%
where the time goes in v3:
time: 44.8 us; the launch traced here: 44.6 us
  Pallas kernels  18 us (40%)
  waiting for transfers between devices  13.9 us (31%)
  starting transfers between devices  10.9 us (24%)
  local copies, waits for them, and re-layouts  1.04 us (2%)
  between operations  0.69 us (2%)
    pallas_call x1, Pallas kernels, sweep_call(): pl.pallas_call(functools.partial(sweep_kernel, (extent, planes, pairs, to...  8.02 us
    pallas_call x1, Pallas kernels, product_call(): pl.pallas_call(functools.partial(product_kernel, row_tiles, pairs), out_s...  7.2 us
    ppermute x1, waiting for transfers between devices, on_device(): across = lax.ppermute(near, 'section', flip(2))  4.7 us
    ppermute x1, waiting for transfers between devices, on_device(): opposite = lax.ppermute(summed, 'narrow', flip(2))  4.5 us
    ppermute x1, starting transfers between devices, on_device(): summed = kept + lax.ppermute(away, 'narrow', flip(1))  3.12 us
    pallas_call x1, Pallas kernels, pick_call(): pl.pallas_call(functools.partial(pick_kernel, pairs, count, block_of), ou...  2.74 us
    ppermute x1, starting transfers between devices, on_device(): opposite = lax.ppermute(summed, 'narrow', flip(2))  2.66 us
    ppermute x1, starting transfers between devices, on_device(): lax.ppermute(to_both, ('wide', 'narrow'), [(i, i ^ 5) for i in range(8)])  1.91 us
  transfers between devices with their start and end apart: 8, of which 6 were waited for; matrix products, arithmetic and copies ran while one was open for 0% of the time, Pallas kernels for 6%

profile of v3, /device:TPU:0, one launch (start us, length us, event | category | flops | bytes accessed | tf_op | source)
XLA Modules:
  0.0 44.6 jit_solution(6673496672423302426)
XLA Ops:
  0.7 8.0 %sweep.1 = (f32[48,4,128]{2,1,0:T(4,128)}, f32[21,48,128]{2,1,0:T(8,128)}) custom-call(s32[2,4]{1,0:T(2,128)} %bitcast.15, f32[8]{0:T(128)} %refs_1_.1, f32[8]{0:T(128)} %refs_2_.1, f32[1]{0:T(128)S(6)} %copy.12.refs_3_, f32[12,8,2304]{2,1,0:T(8,128)} %bitcast.12, f32[12,1,2304]{2,1,0:T(1,128)} %bitcast.13, bf16[384,512]{1,0:T(8,128)(2,1)} %constant.8.clone.refs_6_, ...), custom_call_target="tpu_custom_call" | custom-call | flops 8000000000 | bytes 4000000 | tf_op jit(solution)/shard_map/sweep/pallas_call | solution.py:246
  8.7 3.1 %collective-permute-start = (f32[48,4,128]{2,1,0:T(4,128)}, f32[48,4,128]{2,1,0:T(4,128)S(1)}, u32[]{:S(2)}, u32[]{:S(2)}) collective-permute-start(f32[48,4,128]{2,1,0:T(4,128)} %get-tuple-element.12), channel_id=1, source_target_pairs={{0,1},{1,0},{2,3},{3,2},{4,5},{5,4},{6,7},{7,6},{8,9},{9,8},{10,11... | collective-permute-start | bytes 294920 | tf_op jit(solution)/shard_map/ppermute | solution.py:420
  11.8 0.0 copy-start
  11.8 1.0 %copy-done = f32[21,48,128]{2,1,0:T(8,128)S(1)} copy-done((f32[21,48,128]{2,1,0:T(8,128)S(1)}, f32[21,48,128]{2,1,0:T(8,128)}, u32[]{:S(2)}) %copy-start) | copy-done | bytes 516120
  12.8 2.7 %pick.1 = f32[48,4,128]{2,1,0:T(4,128)S(1)} custom-call(f32[21,48,128]{2,1,0:T(8,128)S(1)} %copy-done), custom_call_target="tpu_custom_call" | custom-call | flops 4000000000 | bytes 1000000 | tf_op jit(solution)/shard_map/pick/pallas_call | solution.py:266
  15.6 0.0 collective-permute-done
  15.6 2.7 %collective-permute-start.1 = (f32[48,4,128]{2,1,0:T(4,128)S(1)}, f32[48,4,128]{2,1,0:T(4,128)S(1)}, u32[]{:S(2)}, u32[]{:S(2)}) collective-permute-start(f32[48,4,128]{2,1,0:T(4,128)S(1)} %add.3.near_ref), channel_id=1, source_target_pairs={{0,2},{1,3},{2,0},{3,1},{4,6},{5,7},{6,4},{7,5},{8,10},{9,11},{10,... | collective-permute-start | bytes 294920 | tf_op jit(solution)/shard_map/ppermute | solution.py:421
  18.3 4.5 %collective-permute-done.1.far_ref = f32[48,4,128]{2,1,0:T(4,128)S(1)} collective-permute-done((f32[48,4,128]{2,1,0:T(4,128)S(1)}, f32[48,4,128]{2,1,0:T(4,128)S(1)}, u32[]{:S(2)}, u32[]{:S(2)}) %collective-permute-start.1) | collective-permute-done | bytes 98336 | tf_op jit(solution)/shard_map/ppermute | solution.py:421
  22.8 1.6 %collective-permute-start.2 = (f32[30,4,128]{2,1,0:T(4,128)S(1)}, f32[30,4,128]{2,1,0:T(4,128)S(1)}, u32[]{:S(2)}, u32[]{:S(2)}) collective-permute-start(f32[30,4,128]{2,1,0:T(4,128)S(1)} %get-tuple-element.14), channel_id=1, source_target_pairs={{0,4},{4,0},{1,5},{5,1},{2,6},{6,2},{3,7},{7,3},{8,12},{12,8},{9,1... | collective-permute-start | bytes 184328 | tf_op jit(solution)/shard_map/ppermute | solution.py:423
  24.5 0.0 collective-permute-start.3
  24.5 1.9 %collective-permute-start.4 = (f32[30,4,128]{2,1,0:T(4,128)S(1)}, f32[30,4,128]{2,1,0:T(4,128)S(1)}, u32[]{:S(2)}, u32[]{:S(2)}) collective-permute-start(f32[30,4,128]{2,1,0:T(4,128)S(1)} %get-tuple-element.16), channel_id=1, source_target_pairs={{0,5},{1,4},{2,7},{3,6},{4,1},{5,0},{6,3},{7,2},{8,13},{9,12},{10,... | collective-permute-start | bytes 184328 | tf_op jit(solution)/shard_map/ppermute | solution.py:425
  26.4 0.7 %collective-permute-done.2 = f32[30,4,128]{2,1,0:T(4,128)S(1)} collective-permute-done((f32[30,4,128]{2,1,0:T(4,128)S(1)}, f32[30,4,128]{2,1,0:T(4,128)S(1)}, u32[]{:S(2)}, u32[]{:S(2)}) %collective-permute-start.2) | collective-permute-done | bytes 61472 | tf_op jit(solution)/shard_map/ppermute | solution.py:423
  27.1 1.6 %collective-permute-done.3 = f32[30,4,128]{2,1,0:T(4,128)S(1)} collective-permute-done((f32[30,4,128]{2,1,0:T(4,128)S(1)}, f32[30,4,128]{2,1,0:T(4,128)S(1)}, u32[]{:S(2)}, u32[]{:S(2)}) %collective-permute-start.3) | collective-permute-done | bytes 61472 | tf_op jit(solution)/shard_map/ppermute | solution.py:424
  28.7 0.9 %collective-permute-done.4 = f32[30,4,128]{2,1,0:T(4,128)S(1)} collective-permute-done((f32[30,4,128]{2,1,0:T(4,128)S(1)}, f32[30,4,128]{2,1,0:T(4,128)S(1)}, u32[]{:S(2)}, u32[]{:S(2)}) %collective-permute-start.4) | collective-permute-done | bytes 61472 | tf_op jit(solution)/shard_map/ppermute | solution.py:425
  29.6 0.1 pad_maximum_fusion.own_ref
  29.7 1.6 %collective-permute-start.5 = (f32[4,30,4,128]{3,2,1,0:T(4,128)S(1)}, f32[4,30,4,128]{3,2,1,0:T(4,128)S(1)}, u32[]{:S(2)}, u32[]{:S(2)}) collective-permute-start(f32[4,30,4,128]{3,2,1,0:T(4,128)S(1)} %pad_maximum_fusion.own_ref), channel_id=1, source_target_pairs={{0,16},{8,24},{16,0},{24,8},{1,17},{9,25},{17,1},{25,9},{2,18},{10... | collective-permute-start | bytes 737288 | tf_op jit(solution)/shard_map/ppermute | solution.py:427
  31.2 0.0 collective-permute-start.6
  31.2 4.7 %collective-permute-done.5.across_ref = f32[4,30,4,128]{3,2,1,0:T(4,128)S(1)} collective-permute-done((f32[4,30,4,128]{3,2,1,0:T(4,128)S(1)}, f32[4,30,4,128]{3,2,1,0:T(4,128)S(1)}, u32[]{:S(2)}, u32[]{:S(2)}) %collective-permute-start.5) | collective-permute-done | bytes 245792 | tf_op jit(solution)/shard_map/ppermute | solution.py:427
  35.9 0.0 collective-permute-start.7
  35.9 0.0 collective-permute-done.6.core_ref
  35.9 1.5 %collective-permute-done.7.far_ref = f32[4,30,4,128]{3,2,1,0:T(4,128)S(1)} collective-permute-done((f32[4,30,4,128]{3,2,1,0:T(4,128)S(1)}, f32[4,30,4,128]{3,2,1,0:T(4,128)S(1)}, u32[]{:S(2)}, u32[]{:S(2)}) %collective-permute-start.7) | collective-permute-done | bytes 245792 | tf_op jit(solution)/shard_map/ppermute | solution.py:429
  37.4 7.2 %product.1 = f32[768,6144]{1,0:T(8,128)} custom-call(f32[4,30,4,128]{3,2,1,0:T(4,128)S(1)} %pad_maximum_fusion.own_ref, f32[4,30,4,128]{3,2,1,0:T(4,128)S(1)} %collective-permute-done.5.across_ref, f32[4,30,4,128]{3,2,1,0:T(4,128)S(1)} %collective-permute-done.6.core_ref, f32[4,30,4,128]{3,2,1,0:T(4,128)S(1)} %collective-permute-done.7.far_ref), custom_call_target="tpu_custom_call" | custom-call | tf_op jit(solution)/shard_map/product/pallas_call | solution.py:354
  (2 shorter events, 0.1 us)
Async XLA Ops:
  8.7 6.9 %collective-permute-start = (f32[48,4,128]{2,1,0:T(4,128)}, f32[48,4,128]{2,1,0:T(4,128)S(1)}, u32[]{:S(2)}, u32[]{:S(2)}) collective-permute-start(f32[48,4,128]{2,1,0:T(4,128)} %get-tuple-element.12), channel_id=1, source_target_pairs={{0,1},{1,0},{2,3},{3,2},{4,5},{5,4},{6,7},{7,6},{8,9},{9,8},{10,11... | collective-permute-start | bytes 294920 | tf_op jit(solution)/shard_map/ppermute | solution.py:420
  11.8 1.0 %copy-start = (f32[21,48,128]{2,1,0:T(8,128)S(1)}, f32[21,48,128]{2,1,0:T(8,128)}, u32[]{:S(2)}) copy-start(f32[21,48,128]{2,1,0:T(8,128)} %get-tuple-element.11.refs_0_) | copy-start | bytes 1548292
  15.6 7.2 %collective-permute-start.1 = (f32[48,4,128]{2,1,0:T(4,128)S(1)}, f32[48,4,128]{2,1,0:T(4,128)S(1)}, u32[]{:S(2)}, u32[]{:S(2)}) collective-permute-start(f32[48,4,128]{2,1,0:T(4,128)S(1)} %add.3.near_ref), channel_id=1, source_target_pairs={{0,2},{1,3},{2,0},{3,1},{4,6},{5,7},{6,4},{7,5},{8,10},{9,11},{10,... | collective-permute-start | bytes 294920 | tf_op jit(solution)/shard_map/ppermute | solution.py:421
  22.8 4.3 %collective-permute-start.2 = (f32[30,4,128]{2,1,0:T(4,128)S(1)}, f32[30,4,128]{2,1,0:T(4,128)S(1)}, u32[]{:S(2)}, u32[]{:S(2)}) collective-permute-start(f32[30,4,128]{2,1,0:T(4,128)S(1)} %get-tuple-element.14), channel_id=1, source_target_pairs={{0,4},{4,0},{1,5},{5,1},{2,6},{6,2},{3,7},{7,3},{8,12},{12,8},{9,1... | collective-permute-start | bytes 184328 | tf_op jit(solution)/shard_map/ppermute | solution.py:423
  24.5 4.2 %collective-permute-start.3 = (f32[30,4,128]{2,1,0:T(4,128)S(1)}, f32[30,4,128]{2,1,0:T(4,128)S(1)}, u32[]{:S(2)}, u32[]{:S(2)}) collective-permute-start(f32[30,4,128]{2,1,0:T(4,128)S(1)} %get-tuple-element.15), channel_id=1, source_target_pairs={{0,1},{1,0},{2,3},{3,2},{4,5},{5,4},{6,7},{7,6},{8,9},{9,8},{10,11... | collective-permute-start | bytes 184328 | tf_op jit(solution)/shard_map/ppermute | solution.py:424
  24.5 5.1 %collective-permute-start.4 = (f32[30,4,128]{2,1,0:T(4,128)S(1)}, f32[30,4,128]{2,1,0:T(4,128)S(1)}, u32[]{:S(2)}, u32[]{:S(2)}) collective-permute-start(f32[30,4,128]{2,1,0:T(4,128)S(1)} %get-tuple-element.16), channel_id=1, source_target_pairs={{0,5},{1,4},{2,7},{3,6},{4,1},{5,0},{6,3},{7,2},{8,13},{9,12},{10,... | collective-permute-start | bytes 184328 | tf_op jit(solution)/shard_map/ppermute | solution.py:425
  29.7 6.3 %collective-permute-start.5 = (f32[4,30,4,128]{3,2,1,0:T(4,128)S(1)}, f32[4,30,4,128]{3,2,1,0:T(4,128)S(1)}, u32[]{:S(2)}, u32[]{:S(2)}) collective-permute-start(f32[4,30,4,128]{3,2,1,0:T(4,128)S(1)} %pad_maximum_fusion.own_ref), channel_id=1, source_target_pairs={{0,16},{8,24},{16,0},{24,8},{1,17},{9,25},{17,1},{25,9},{2,18},{10... | collective-permute-start | bytes 737288 | tf_op jit(solution)/shard_map/ppermute | solution.py:427
  31.2 4.7 %collective-permute-start.6 = (f32[4,30,4,128]{3,2,1,0:T(4,128)S(1)}, f32[4,30,4,128]{3,2,1,0:T(4,128)S(1)}, u32[]{:S(2)}, u32[]{:S(2)}) collective-permute-start(f32[4,30,4,128]{3,2,1,0:T(4,128)S(1)} %pad_maximum_fusion.own_ref), channel_id=1, source_target_pairs={{0,8},{8,0},{16,24},{24,16},{1,9},{9,1},{17,25},{25,17},{2,10},{10... | collective-permute-start | bytes 737288 | tf_op jit(solution)/shard_map/ppermute | solution.py:428
  35.9 1.5 %collective-permute-start.7 = (f32[4,30,4,128]{3,2,1,0:T(4,128)S(1)}, f32[4,30,4,128]{3,2,1,0:T(4,128)S(1)}, u32[]{:S(2)}, u32[]{:S(2)}) collective-permute-start(f32[4,30,4,128]{3,2,1,0:T(4,128)S(1)} %collective-permute-done.5.across_ref), channel_id=1, source_target_pairs={{0,8},{8,0},{16,24},{24,16},{1,9},{9,1},{17,25},{25,17},{2,10},{10... | collective-permute-start | bytes 737288 | tf_op jit(solution)/shard_map/ppermute | solution.py:429

commit v4 on v3

--- a/solution.py
+++ b/solution.py
@@ -111,18 +111,17 @@
         finish(places[2], ids[2], third)
         return carry
 
-    lax.fori_loop(0, count // 3, three, 0, unroll=8)
+    lax.fori_loop(0, count // 3, three, 0, unroll=16)
 
 
 def sweep_kernel(
     sizes,
     *refs,
 ):
-    given, (out_ref, kept_ref), held = refs[:11], refs[11:13], refs[13:24]
-    table_ref, density_ref, fold_ref, *picking, sems, store_sem = refs[24:]
-    store = pltpu.make_async_copy(table_ref, kept_ref, store_sem)
+    given, (out_ref, table_ref), held = refs[:11], refs[11:13], refs[13:24]
+    density_ref, fold_ref, *picking, sems = refs[24:]
     loads = [pltpu.make_async_copy(source, target, sems.at[i]) for i, (source, target) in enumerate(zip(given, held))]
-    for load in loads:
+    for load in loads[4:6] + loads[:4] + loads[6:]:
         load.start()
     bands_ref, valence_energy_ref, conduction_energy_ref, frequency_ref, *held = held
     valence_ref, conduction_ref, z_high_ref, z_low_ref, y_ref, x_ref, index_ref = held
@@ -209,9 +208,7 @@
     for i in range(table_ref.shape[0] - per_plane - 1):
         some = min(rows, blocks - i * rows)
         table_ref[per_plane + 1 + i, pl.ds(0, some), :] = index_ref[pl.ds(i * rows, some), :].astype(F32)
-    store.start()
     pick_blocks(pairs, count, block_of(), table_ref, out_ref, *picking)
-    store.wait()
 
 
 def pick_kernel(pairs, count, block_of, *refs):
@@ -224,6 +221,7 @@
 
 VMEM = pl.BlockSpec(memory_space=pltpu.VMEM)
 HBM = pl.BlockSpec(memory_space=pltpu.HBM)
+ANY = pl.BlockSpec(memory_space=pl.ANY)
 
 
 def sweep_call(bands, valence_energy, conduction_energy, frequency, valence, conduction, index, total_pairs, count, block_of):
@@ -246,20 +244,20 @@
     return pl.pallas_call(
         functools.partial(sweep_kernel, (extent, planes, pairs, total_pairs, count, block_of)),
         out_shape=[jax.ShapeDtypeStruct((count, pairs, LANES), F32), table],
-        in_specs=[HBM] * (len(scalars) + len(operands)),
-        out_specs=[VMEM, HBM],
+        in_specs=[HBM] * 3 + [ANY] + [HBM] * len(operands),
+        out_specs=[VMEM, VMEM],
         scratch_shapes=[pltpu.SMEM(a.shape, a.dtype) for a in scalars]
         + [pltpu.VMEM(a.shape, a.dtype) for a in operands]
         + [
-            pltpu.VMEM(table.shape, F32),
             pltpu.VMEM((3, groups * rows, LANES), F32),
             pltpu.VMEM((2, extent // 4, rows, LANES), F32),
         ]
         + pick_scratch(blocks, rows, area)
-        + [pltpu.SemaphoreType.DMA((len(scalars) + len(operands),)), pltpu.SemaphoreType.DMA],
+        + [pltpu.SemaphoreType.DMA((len(scalars) + len(operands),))],
+        compiler_params=pltpu.CompilerParams(vmem_limit_bytes=32 << 20),
         cost_estimate=pl.CostEstimate(flops=8_000_000_000, bytes_accessed=4_000_000, transcendentals=0),
         name="sweep",
-    )(*scalars, *operands)
+    )(*(a if a is frequency else pltpu.with_memory_space_constraint(a, pltpu.HBM) for a in (*scalars, *operands)))
 
 
 def pick_call(table, blocks, area, pairs, count, block_of):

time: 44.8 us -> 43.3 us (0.967)
  local copies, waits for them, and re-layouts: 1.04 us -> 0 us
  Pallas kernels: 18 us -> 17 us
    unnamed x2 -> x0, local copies, waits for them, and re-layouts: 1.04 us -> none
    pallas_call x1, Pallas kernels: 8.02 us -> 7.19 us  [sweep_call(): pl.pallas_call(functools.partial(sweep_kernel, (extent, planes, pairs, to...]
    ppermute x1, waiting for transfers between devices: 0.9 us -> 1.36 us  [on_device(): lax.ppermute(to_both, ('wide', 'narrow'), [(i, i ^ 5) for i in range(8)])]
    ppermute x1, starting transfers between devices: 0.01 us -> 0.46 us  [on_device(): from_narrow = lax.ppermute(to_narrow, 'narrow', flip(1))]
  transfers between devices with their start and end apart: 8 -> 8, of which waited for: 6 -> 7; matrix products, arithmetic and copies ran while one was open for 0% -> 0% of each run, Pallas kernels for 6% -> 6%
where the time goes in v4:
time: 43.3 us; the launch traced here: 43.1 us
  Pallas kernels  17 us (39%)
  waiting for transfers between devices  14.3 us (33%)
  starting transfers between devices  11.1 us (26%)
  between operations  0.68 us (2%)
    pallas_call x1, Pallas kernels, product_call(): pl.pallas_call(functools.partial(product_kernel, row_tiles, pairs), out_s...  7.2 us
    pallas_call x1, Pallas kernels, sweep_call(): pl.pallas_call(functools.partial(sweep_kernel, (extent, planes, pairs, to...  7.19 us
    ppermute x1, waiting for transfers between devices, on_device(): across = lax.ppermute(near, 'section', flip(2))  4.7 us
    ppermute x1, waiting for transfers between devices, on_device(): opposite = lax.ppermute(summed, 'narrow', flip(2))  4.18 us
    ppermute x1, starting transfers between devices, on_device(): summed = kept + lax.ppermute(away, 'narrow', flip(1))  3.12 us
    ppermute x1, starting transfers between devices, on_device(): opposite = lax.ppermute(summed, 'narrow', flip(2))  2.9 us
    pallas_call x1, Pallas kernels, pick_call(): pl.pallas_call(functools.partial(pick_kernel, pairs, count, block_of), ou...  2.53 us
    ppermute x1, starting transfers between devices, on_device(): from_wide = lax.ppermute(to_wide, 'wide', [(0, 1), (1, 0)])  1.58 us
  transfers between devices with their start and end apart: 8, of which 7 were waited for; matrix products, arithmetic and copies ran while one was open for 0% of the time, Pallas kernels for 6%

profile of v4, /device:TPU:0, one launch (start us, length us, event | category | flops | bytes accessed | tf_op | source)
XLA Modules:
  0.0 43.1 jit_solution(12152085006977478926)
XLA Ops:
  0.7 7.2 %sweep.1 = (f32[48,4,128]{2,1,0:T(4,128)S(1)}, f32[21,48,128]{2,1,0:T(8,128)S(1)}) custom-call(s32[2,4]{1,0:T(2,128)} %bitcast.15, f32[8]{0:T(128)} %refs_1_.1, f32[8]{0:T(128)} %refs_2_.1, f32[1]{0:T(128)S(6)} %copy.12.refs_3_, f32[12,8,2304]{2,1,0:T(8,128)} %bitcast.12, f32[12,1,2304]{2,1,0:T(1,128)} %bitcast.13, bf16[384,512]{1,0:T(8,128)(2,1)} %constant.8.clone.refs_6_, ...), custom_call_target="tpu_custom_call" | custom-call | flops 8000000000 | bytes 4000000 | tf_op jit(solution)/shard_map/sweep/pallas_call | solution.py:244
  7.8 3.1 %collective-permute-start = (f32[48,4,128]{2,1,0:T(4,128)S(1)}, f32[48,4,128]{2,1,0:T(4,128)S(1)}, u32[]{:S(2)}, u32[]{:S(2)}) collective-permute-start(f32[48,4,128]{2,1,0:T(4,128)S(1)} %get-tuple-element.12), channel_id=1, source_target_pairs={{0,1},{1,0},{2,3},{3,2},{4,5},{5,4},{6,7},{7,6},{8,9},{9,8},{10,11... | collective-permute-start | bytes 294920 | tf_op jit(solution)/shard_map/ppermute | solution.py:418
  11.0 2.5 %pick.1 = f32[48,4,128]{2,1,0:T(4,128)S(1)} custom-call(f32[21,48,128]{2,1,0:T(8,128)S(1)} %get-tuple-element.11.refs_0_), custom_call_target="tpu_custom_call" | custom-call | flops 4000000000 | bytes 1000000 | tf_op jit(solution)/shard_map/pick/pallas_call | solution.py:264
  13.5 0.3 collective-permute-done
  13.8 2.9 %collective-permute-start.1 = (f32[48,4,128]{2,1,0:T(4,128)S(1)}, f32[48,4,128]{2,1,0:T(4,128)S(1)}, u32[]{:S(2)}, u32[]{:S(2)}) collective-permute-start(f32[48,4,128]{2,1,0:T(4,128)S(1)} %add.3.near_ref), channel_id=1, source_target_pairs={{0,2},{1,3},{2,0},{3,1},{4,6},{5,7},{6,4},{7,5},{8,10},{9,11},{10,... | collective-permute-start | bytes 294920 | tf_op jit(solution)/shard_map/ppermute | solution.py:419
  16.7 4.2 %collective-permute-done.1.far_ref = f32[48,4,128]{2,1,0:T(4,128)S(1)} collective-permute-done((f32[48,4,128]{2,1,0:T(4,128)S(1)}, f32[48,4,128]{2,1,0:T(4,128)S(1)}, u32[]{:S(2)}, u32[]{:S(2)}) %collective-permute-start.1) | collective-permute-done | bytes 98336 | tf_op jit(solution)/shard_map/ppermute | solution.py:419
  20.9 1.6 %collective-permute-start.2 = (f32[30,4,128]{2,1,0:T(4,128)S(1)}, f32[30,4,128]{2,1,0:T(4,128)S(1)}, u32[]{:S(2)}, u32[]{:S(2)}) collective-permute-start(f32[30,4,128]{2,1,0:T(4,128)S(1)} %get-tuple-element.14), channel_id=1, source_target_pairs={{0,4},{4,0},{1,5},{5,1},{2,6},{6,2},{3,7},{7,3},{8,12},{12,8},{9,1... | collective-permute-start | bytes 184328 | tf_op jit(solution)/shard_map/ppermute | solution.py:421
  22.5 0.5 %collective-permute-start.3 = (f32[30,4,128]{2,1,0:T(4,128)S(1)}, f32[30,4,128]{2,1,0:T(4,128)S(1)}, u32[]{:S(2)}, u32[]{:S(2)}) collective-permute-start(f32[30,4,128]{2,1,0:T(4,128)S(1)} %get-tuple-element.15), channel_id=1, source_target_pairs={{0,1},{1,0},{2,3},{3,2},{4,5},{5,4},{6,7},{7,6},{8,9},{9,8},{10,11... | collective-permute-start | bytes 184328 | tf_op jit(solution)/shard_map/ppermute | solution.py:422
  23.0 1.5 %collective-permute-start.4 = (f32[30,4,128]{2,1,0:T(4,128)S(1)}, f32[30,4,128]{2,1,0:T(4,128)S(1)}, u32[]{:S(2)}, u32[]{:S(2)}) collective-permute-start(f32[30,4,128]{2,1,0:T(4,128)S(1)} %get-tuple-element.16), channel_id=1, source_target_pairs={{0,5},{1,4},{2,7},{3,6},{4,1},{5,0},{6,3},{7,2},{8,13},{9,12},{10,... | collective-permute-start | bytes 184328 | tf_op jit(solution)/shard_map/ppermute | solution.py:423
  24.5 0.8 %collective-permute-done.2 = f32[30,4,128]{2,1,0:T(4,128)S(1)} collective-permute-done((f32[30,4,128]{2,1,0:T(4,128)S(1)}, f32[30,4,128]{2,1,0:T(4,128)S(1)}, u32[]{:S(2)}, u32[]{:S(2)}) %collective-permute-start.2) | collective-permute-done | bytes 61472 | tf_op jit(solution)/shard_map/ppermute | solution.py:421
  25.3 1.5 %collective-permute-done.3 = f32[30,4,128]{2,1,0:T(4,128)S(1)} collective-permute-done((f32[30,4,128]{2,1,0:T(4,128)S(1)}, f32[30,4,128]{2,1,0:T(4,128)S(1)}, u32[]{:S(2)}, u32[]{:S(2)}) %collective-permute-start.3) | collective-permute-done | bytes 61472 | tf_op jit(solution)/shard_map/ppermute | solution.py:422
  26.7 1.4 %collective-permute-done.4 = f32[30,4,128]{2,1,0:T(4,128)S(1)} collective-permute-done((f32[30,4,128]{2,1,0:T(4,128)S(1)}, f32[30,4,128]{2,1,0:T(4,128)S(1)}, u32[]{:S(2)}, u32[]{:S(2)}) %collective-permute-start.4) | collective-permute-done | bytes 61472 | tf_op jit(solution)/shard_map/ppermute | solution.py:423
  28.1 0.1 pad_maximum_fusion.own_ref
  28.2 1.6 %collective-permute-start.5 = (f32[4,30,4,128]{3,2,1,0:T(4,128)S(1)}, f32[4,30,4,128]{3,2,1,0:T(4,128)S(1)}, u32[]{:S(2)}, u32[]{:S(2)}) collective-permute-start(f32[4,30,4,128]{3,2,1,0:T(4,128)S(1)} %pad_maximum_fusion.own_ref), channel_id=1, source_target_pairs={{0,16},{8,24},{16,0},{24,8},{1,17},{9,25},{17,1},{25,9},{2,18},{10... | collective-permute-start | bytes 737288 | tf_op jit(solution)/shard_map/ppermute | solution.py:425
  29.7 0.0 collective-permute-start.6
  29.7 4.7 %collective-permute-done.5.across_ref = f32[4,30,4,128]{3,2,1,0:T(4,128)S(1)} collective-permute-done((f32[4,30,4,128]{3,2,1,0:T(4,128)S(1)}, f32[4,30,4,128]{3,2,1,0:T(4,128)S(1)}, u32[]{:S(2)}, u32[]{:S(2)}) %collective-permute-start.5) | collective-permute-done | bytes 245792 | tf_op jit(solution)/shard_map/ppermute | solution.py:425
  34.4 0.0 collective-permute-start.7
  34.4 0.0 collective-permute-done.6.core_ref
  34.4 1.5 %collective-permute-done.7.far_ref = f32[4,30,4,128]{3,2,1,0:T(4,128)S(1)} collective-permute-done((f32[4,30,4,128]{3,2,1,0:T(4,128)S(1)}, f32[4,30,4,128]{3,2,1,0:T(4,128)S(1)}, u32[]{:S(2)}, u32[]{:S(2)}) %collective-permute-start.7) | collective-permute-done | bytes 245792 | tf_op jit(solution)/shard_map/ppermute | solution.py:427
  35.9 7.2 %product.1 = f32[768,6144]{1,0:T(8,128)} custom-call(f32[4,30,4,128]{3,2,1,0:T(4,128)S(1)} %pad_maximum_fusion.own_ref, f32[4,30,4,128]{3,2,1,0:T(4,128)S(1)} %collective-permute-done.5.across_ref, f32[4,30,4,128]{3,2,1,0:T(4,128)S(1)} %collective-permute-done.6.core_ref, f32[4,30,4,128]{3,2,1,0:T(4,128)S(1)} %collective-permute-done.7.far_ref), custom_call_target="tpu_custom_call" | custom-call | tf_op jit(solution)/shard_map/product/pallas_call | solution.py:352
  (2 shorter events, 0.1 us)
Async XLA Ops:
  7.8 5.9 %collective-permute-start = (f32[48,4,128]{2,1,0:T(4,128)S(1)}, f32[48,4,128]{2,1,0:T(4,128)S(1)}, u32[]{:S(2)}, u32[]{:S(2)}) collective-permute-start(f32[48,4,128]{2,1,0:T(4,128)S(1)} %get-tuple-element.12), channel_id=1, source_target_pairs={{0,1},{1,0},{2,3},{3,2},{4,5},{5,4},{6,7},{7,6},{8,9},{9,8},{10,11... | collective-permute-start | bytes 294920 | tf_op jit(solution)/shard_map/ppermute | solution.py:418
  13.8 7.1 %collective-permute-start.1 = (f32[48,4,128]{2,1,0:T(4,128)S(1)}, f32[48,4,128]{2,1,0:T(4,128)S(1)}, u32[]{:S(2)}, u32[]{:S(2)}) collective-permute-start(f32[48,4,128]{2,1,0:T(4,128)S(1)} %add.3.near_ref), channel_id=1, source_target_pairs={{0,2},{1,3},{2,0},{3,1},{4,6},{5,7},{6,4},{7,5},{8,10},{9,11},{10,... | collective-permute-start | bytes 294920 | tf_op jit(solution)/shard_map/ppermute | solution.py:419
  20.9 4.3 %collective-permute-start.2 = (f32[30,4,128]{2,1,0:T(4,128)S(1)}, f32[30,4,128]{2,1,0:T(4,128)S(1)}, u32[]{:S(2)}, u32[]{:S(2)}) collective-permute-start(f32[30,4,128]{2,1,0:T(4,128)S(1)} %get-tuple-element.14), channel_id=1, source_target_pairs={{0,4},{4,0},{1,5},{5,1},{2,6},{6,2},{3,7},{7,3},{8,12},{12,8},{9,1... | collective-permute-start | bytes 184328 | tf_op jit(solution)/shard_map/ppermute | solution.py:421
  22.5 4.2 %collective-permute-start.3 = (f32[30,4,128]{2,1,0:T(4,128)S(1)}, f32[30,4,128]{2,1,0:T(4,128)S(1)}, u32[]{:S(2)}, u32[]{:S(2)}) collective-permute-start(f32[30,4,128]{2,1,0:T(4,128)S(1)} %get-tuple-element.15), channel_id=1, source_target_pairs={{0,1},{1,0},{2,3},{3,2},{4,5},{5,4},{6,7},{7,6},{8,9},{9,8},{10,11... | collective-permute-start | bytes 184328 | tf_op jit(solution)/shard_map/ppermute | solution.py:422
  23.0 5.1 %collective-permute-start.4 = (f32[30,4,128]{2,1,0:T(4,128)S(1)}, f32[30,4,128]{2,1,0:T(4,128)S(1)}, u32[]{:S(2)}, u32[]{:S(2)}) collective-permute-start(f32[30,4,128]{2,1,0:T(4,128)S(1)} %get-tuple-element.16), channel_id=1, source_target_pairs={{0,5},{1,4},{2,7},{3,6},{4,1},{5,0},{6,3},{7,2},{8,13},{9,12},{10,... | collective-permute-start | bytes 184328 | tf_op jit(solution)/shard_map/ppermute | solution.py:423
  28.2 6.3 %collective-permute-start.5 = (f32[4,30,4,128]{3,2,1,0:T(4,128)S(1)}, f32[4,30,4,128]{3,2,1,0:T(4,128)S(1)}, u32[]{:S(2)}, u32[]{:S(2)}) collective-permute-start(f32[4,30,4,128]{3,2,1,0:T(4,128)S(1)} %pad_maximum_fusion.own_ref), channel_id=1, source_target_pairs={{0,16},{8,24},{16,0},{24,8},{1,17},{9,25},{17,1},{25,9},{2,18},{10... | collective-permute-start | bytes 737288 | tf_op jit(solution)/shard_map/ppermute | solution.py:425
  29.7 4.7 %collective-permute-start.6 = (f32[4,30,4,128]{3,2,1,0:T(4,128)S(1)}, f32[4,30,4,128]{3,2,1,0:T(4,128)S(1)}, u32[]{:S(2)}, u32[]{:S(2)}) collective-permute-start(f32[4,30,4,128]{3,2,1,0:T(4,128)S(1)} %pad_maximum_fusion.own_ref), channel_id=1, source_target_pairs={{0,8},{8,0},{16,24},{24,16},{1,9},{9,1},{17,25},{25,17},{2,10},{10... | collective-permute-start | bytes 737288 | tf_op jit(solution)/shard_map/ppermute | solution.py:426
  34.4 1.5 %collective-permute-start.7 = (f32[4,30,4,128]{3,2,1,0:T(4,128)S(1)}, f32[4,30,4,128]{3,2,1,0:T(4,128)S(1)}, u32[]{:S(2)}, u32[]{:S(2)}) collective-permute-start(f32[4,30,4,128]{3,2,1,0:T(4,128)S(1)} %collective-permute-done.5.across_ref), channel_id=1, source_target_pairs={{0,8},{8,0},{16,24},{24,16},{1,9},{9,1},{17,25},{25,17},{2,10},{10... | collective-permute-start | bytes 737288 | tf_op jit(solution)/shard_map/ppermute | solution.py:427

commit v5 on v4

--- a/solution.py
+++ b/solution.py
@@ -310,27 +310,31 @@
     sources = (own_ref, across_ref, core_ref, far_ref)
     row_block = rows_ref.shape[0]
 
-    def collect(kind, start):
+    piece = row_tiles // 2
+    width = piece * LANES
+
+    def collect(kind, start, count):
         for i, ref in enumerate(sources):
             for b in range(2):
                 rows = pl.ds((2 * i + b) * pairs, pairs)
-                for r in range(row_tiles):
+                for r in range(count):
                     gather_ref[rows, pl.ds(r * LANES, LANES)] = ref[2 * kind + b, start + r]
-        return gather_ref[...]
+        return gather_ref[:, : count * LANES]
 
     start = jnp.where(section // 2 == wide_pos, narrow_pos * row_tiles, half)
-    high, low = split(-collect((section & 1) ^ parity, start))
+    high, low = split(-collect((section & 1) ^ parity, start, row_tiles))
     high, low = high.astype(F32), low.astype(F32)
     rows_ref[...] = jnp.concatenate([high, high, low, low], axis=0).T.astype(BF16)
 
     def copy_of(step):
-        columns = pl.ds(pl.multiple_of(step * row_block, row_block), row_block)
+        columns = pl.ds(pl.multiple_of(step * width, width), width)
         return pltpu.make_async_copy(value_ref.at[:, columns], out_ref.at[:, columns], sems.at[step])
 
     def one_block(step, carry):
-        high, low = split(collect((step // narrow_count) ^ parity, (step % narrow_count) * row_tiles))
+        per_kind = 2 * narrow_count
+        high, low = split(collect((step // per_kind) ^ parity, (step % per_kind) * piece, piece))
         stacked = jnp.concatenate([high, low, high, low], axis=0)
-        columns = pl.ds(pl.multiple_of(step * row_block, row_block), row_block)
+        columns = pl.ds(pl.multiple_of(step * width, width), width)
         value_ref[:, columns] = jnp.dot(rows_ref[...], stacked, preferred_element_type=F32)
         copy_of(step).start()
         return carry
@@ -339,7 +343,7 @@
         copy_of(step).wait()
         return carry
 
-    steps = 2 * narrow_count
+    steps = 4 * narrow_count
     lax.fori_loop(0, steps, one_block, 0)
     lax.fori_loop(0, steps, wait_block, 0)
 
@@ -358,7 +362,7 @@
             pltpu.VMEM((row_block, 4 * depth), BF16),
             pltpu.VMEM((depth, row_block), F32),
             pltpu.VMEM((row_block, steps * row_block), F32),
-            pltpu.SemaphoreType.DMA((steps,)),
+            pltpu.SemaphoreType.DMA((2 * steps,)),
         ],
         compiler_params=pltpu.CompilerParams(vmem_limit_bytes=40 << 20),
         name="product",

time: 43.3 us -> 43.2 us (level)
  no operation moved by 1% of the time
where the time goes in v5:
time: 43.2 us; the launch traced here: 43 us
  Pallas kernels  16.8 us (39%)
  waiting for transfers between devices  14.3 us (33%)
  starting transfers between devices  11.1 us (26%)
  between operations  0.68 us (2%)
    pallas_call x1, Pallas kernels, sweep_call(): pl.pallas_call(functools.partial(sweep_kernel, (extent, planes, pairs, to...  7.19 us
    pallas_call x1, Pallas kernels, product_call(): pl.pallas_call(functools.partial(product_kernel, row_tiles, pairs), out_s...  7.08 us
    ppermute x1, waiting for transfers between devices, on_device(): across = lax.ppermute(near, 'section', flip(2))  4.7 us
    ppermute x1, waiting for transfers between devices, on_device(): opposite = lax.ppermute(summed, 'narrow', flip(2))  4.18 us
    ppermute x1, starting transfers between devices, on_device(): summed = kept + lax.ppermute(away, 'narrow', flip(1))  3.12 us
    ppermute x1, starting transfers between devices, on_device(): opposite = lax.ppermute(summed, 'narrow', flip(2))  2.9 us
    pallas_call x1, Pallas kernels, pick_call(): pl.pallas_call(functools.partial(pick_kernel, pairs, count, block_of), ou...  2.53 us
    ppermute x1, starting transfers between devices, on_device(): from_wide = lax.ppermute(to_wide, 'wide', [(0, 1), (1, 0)])  1.58 us
  transfers between devices with their start and end apart: 8, of which 7 were waited for; matrix products, arithmetic and copies ran while one was open for 0% of the time, Pallas kernels for 6%

profile of v5, /device:TPU:0, one launch (start us, length us, event | category | flops | bytes accessed | tf_op | source)
XLA Modules:
  0.0 43.0 jit_solution(5945983565094669619)
XLA Ops:
  0.7 7.2 %sweep.1 = (f32[48,4,128]{2,1,0:T(4,128)S(1)}, f32[21,48,128]{2,1,0:T(8,128)S(1)}) custom-call(s32[2,4]{1,0:T(2,128)} %bitcast.15, f32[8]{0:T(128)} %refs_1_.1, f32[8]{0:T(128)} %refs_2_.1, f32[1]{0:T(128)S(6)} %copy.12.refs_3_, f32[12,8,2304]{2,1,0:T(8,128)} %bitcast.12, f32[12,1,2304]{2,1,0:T(1,128)} %bitcast.13, bf16[384,512]{1,0:T(8,128)(2,1)} %constant.8.clone.refs_6_, ...), custom_call_target="tpu_custom_call" | custom-call | flops 8000000000 | bytes 4000000 | tf_op jit(solution)/shard_map/sweep/pallas_call | solution.py:244
  7.8 3.1 %collective-permute-start = (f32[48,4,128]{2,1,0:T(4,128)S(1)}, f32[48,4,128]{2,1,0:T(4,128)S(1)}, u32[]{:S(2)}, u32[]{:S(2)}) collective-permute-start(f32[48,4,128]{2,1,0:T(4,128)S(1)} %get-tuple-element.12), channel_id=1, source_target_pairs={{0,1},{1,0},{2,3},{3,2},{4,5},{5,4},{6,7},{7,6},{8,9},{9,8},{10,11... | collective-permute-start | bytes 294920 | tf_op jit(solution)/shard_map/ppermute | solution.py:422
  11.0 2.5 %pick.1 = f32[48,4,128]{2,1,0:T(4,128)S(1)} custom-call(f32[21,48,128]{2,1,0:T(8,128)S(1)} %get-tuple-element.11.refs_0_), custom_call_target="tpu_custom_call" | custom-call | flops 4000000000 | bytes 1000000 | tf_op jit(solution)/shard_map/pick/pallas_call | solution.py:264
  13.5 0.3 collective-permute-done
  13.8 2.9 %collective-permute-start.1 = (f32[48,4,128]{2,1,0:T(4,128)S(1)}, f32[48,4,128]{2,1,0:T(4,128)S(1)}, u32[]{:S(2)}, u32[]{:S(2)}) collective-permute-start(f32[48,4,128]{2,1,0:T(4,128)S(1)} %add.3.near_ref), channel_id=1, source_target_pairs={{0,2},{1,3},{2,0},{3,1},{4,6},{5,7},{6,4},{7,5},{8,10},{9,11},{10,... | collective-permute-start | bytes 294920 | tf_op jit(solution)/shard_map/ppermute | solution.py:423
  16.7 4.2 %collective-permute-done.1.far_ref = f32[48,4,128]{2,1,0:T(4,128)S(1)} collective-permute-done((f32[48,4,128]{2,1,0:T(4,128)S(1)}, f32[48,4,128]{2,1,0:T(4,128)S(1)}, u32[]{:S(2)}, u32[]{:S(2)}) %collective-permute-start.1) | collective-permute-done | bytes 98336 | tf_op jit(solution)/shard_map/ppermute | solution.py:423
  20.9 1.6 %collective-permute-start.2 = (f32[30,4,128]{2,1,0:T(4,128)S(1)}, f32[30,4,128]{2,1,0:T(4,128)S(1)}, u32[]{:S(2)}, u32[]{:S(2)}) collective-permute-start(f32[30,4,128]{2,1,0:T(4,128)S(1)} %get-tuple-element.14), channel_id=1, source_target_pairs={{0,4},{4,0},{1,5},{5,1},{2,6},{6,2},{3,7},{7,3},{8,12},{12,8},{9,1... | collective-permute-start | bytes 184328 | tf_op jit(solution)/shard_map/ppermute | solution.py:425
  22.5 0.5 %collective-permute-start.3 = (f32[30,4,128]{2,1,0:T(4,128)S(1)}, f32[30,4,128]{2,1,0:T(4,128)S(1)}, u32[]{:S(2)}, u32[]{:S(2)}) collective-permute-start(f32[30,4,128]{2,1,0:T(4,128)S(1)} %get-tuple-element.15), channel_id=1, source_target_pairs={{0,1},{1,0},{2,3},{3,2},{4,5},{5,4},{6,7},{7,6},{8,9},{9,8},{10,11... | collective-permute-start | bytes 184328 | tf_op jit(solution)/shard_map/ppermute | solution.py:426
  23.0 1.5 %collective-permute-start.4 = (f32[30,4,128]{2,1,0:T(4,128)S(1)}, f32[30,4,128]{2,1,0:T(4,128)S(1)}, u32[]{:S(2)}, u32[]{:S(2)}) collective-permute-start(f32[30,4,128]{2,1,0:T(4,128)S(1)} %get-tuple-element.16), channel_id=1, source_target_pairs={{0,5},{1,4},{2,7},{3,6},{4,1},{5,0},{6,3},{7,2},{8,13},{9,12},{10,... | collective-permute-start | bytes 184328 | tf_op jit(solution)/shard_map/ppermute | solution.py:427
  24.5 0.8 %collective-permute-done.2 = f32[30,4,128]{2,1,0:T(4,128)S(1)} collective-permute-done((f32[30,4,128]{2,1,0:T(4,128)S(1)}, f32[30,4,128]{2,1,0:T(4,128)S(1)}, u32[]{:S(2)}, u32[]{:S(2)}) %collective-permute-start.2) | collective-permute-done | bytes 61472 | tf_op jit(solution)/shard_map/ppermute | solution.py:425
  25.3 1.5 %collective-permute-done.3 = f32[30,4,128]{2,1,0:T(4,128)S(1)} collective-permute-done((f32[30,4,128]{2,1,0:T(4,128)S(1)}, f32[30,4,128]{2,1,0:T(4,128)S(1)}, u32[]{:S(2)}, u32[]{:S(2)}) %collective-permute-start.3) | collective-permute-done | bytes 61472 | tf_op jit(solution)/shard_map/ppermute | solution.py:426
  26.7 1.4 %collective-permute-done.4 = f32[30,4,128]{2,1,0:T(4,128)S(1)} collective-permute-done((f32[30,4,128]{2,1,0:T(4,128)S(1)}, f32[30,4,128]{2,1,0:T(4,128)S(1)}, u32[]{:S(2)}, u32[]{:S(2)}) %collective-permute-start.4) | collective-permute-done | bytes 61472 | tf_op jit(solution)/shard_map/ppermute | solution.py:427
  28.1 0.1 pad_maximum_fusion.own_ref
  28.2 1.6 %collective-permute-start.5 = (f32[4,30,4,128]{3,2,1,0:T(4,128)S(1)}, f32[4,30,4,128]{3,2,1,0:T(4,128)S(1)}, u32[]{:S(2)}, u32[]{:S(2)}) collective-permute-start(f32[4,30,4,128]{3,2,1,0:T(4,128)S(1)} %pad_maximum_fusion.own_ref), channel_id=1, source_target_pairs={{0,16},{8,24},{16,0},{24,8},{1,17},{9,25},{17,1},{25,9},{2,18},{10... | collective-permute-start | bytes 737288 | tf_op jit(solution)/shard_map/ppermute | solution.py:429
  29.7 0.0 collective-permute-start.6
  29.7 4.7 %collective-permute-done.5.across_ref = f32[4,30,4,128]{3,2,1,0:T(4,128)S(1)} collective-permute-done((f32[4,30,4,128]{3,2,1,0:T(4,128)S(1)}, f32[4,30,4,128]{3,2,1,0:T(4,128)S(1)}, u32[]{:S(2)}, u32[]{:S(2)}) %collective-permute-start.5) | collective-permute-done | bytes 245792 | tf_op jit(solution)/shard_map/ppermute | solution.py:429
  34.4 0.0 collective-permute-start.7
  34.4 0.0 collective-permute-done.6.core_ref
  34.4 1.5 %collective-permute-done.7.far_ref = f32[4,30,4,128]{3,2,1,0:T(4,128)S(1)} collective-permute-done((f32[4,30,4,128]{3,2,1,0:T(4,128)S(1)}, f32[4,30,4,128]{3,2,1,0:T(4,128)S(1)}, u32[]{:S(2)}, u32[]{:S(2)}) %collective-permute-start.7) | collective-permute-done | bytes 245792 | tf_op jit(solution)/shard_map/ppermute | solution.py:431
  35.9 7.1 %product.1 = f32[768,6144]{1,0:T(8,128)} custom-call(f32[4,30,4,128]{3,2,1,0:T(4,128)S(1)} %pad_maximum_fusion.own_ref, f32[4,30,4,128]{3,2,1,0:T(4,128)S(1)} %collective-permute-done.5.across_ref, f32[4,30,4,128]{3,2,1,0:T(4,128)S(1)} %collective-permute-done.6.core_ref, f32[4,30,4,128]{3,2,1,0:T(4,128)S(1)} %collective-permute-done.7.far_ref), custom_call_target="tpu_custom_call" | custom-call | tf_op jit(solution)/shard_map/product/pallas_call | solution.py:356
  (2 shorter events, 0.1 us)
Async XLA Ops:
  7.8 5.9 %collective-permute-start = (f32[48,4,128]{2,1,0:T(4,128)S(1)}, f32[48,4,128]{2,1,0:T(4,128)S(1)}, u32[]{:S(2)}, u32[]{:S(2)}) collective-permute-start(f32[48,4,128]{2,1,0:T(4,128)S(1)} %get-tuple-element.12), channel_id=1, source_target_pairs={{0,1},{1,0},{2,3},{3,2},{4,5},{5,4},{6,7},{7,6},{8,9},{9,8},{10,11... | collective-permute-start | bytes 294920 | tf_op jit(solution)/shard_map/ppermute | solution.py:422
  13.8 7.1 %collective-permute-start.1 = (f32[48,4,128]{2,1,0:T(4,128)S(1)}, f32[48,4,128]{2,1,0:T(4,128)S(1)}, u32[]{:S(2)}, u32[]{:S(2)}) collective-permute-start(f32[48,4,128]{2,1,0:T(4,128)S(1)} %add.3.near_ref), channel_id=1, source_target_pairs={{0,2},{1,3},{2,0},{3,1},{4,6},{5,7},{6,4},{7,5},{8,10},{9,11},{10,... | collective-permute-start | bytes 294920 | tf_op jit(solution)/shard_map/ppermute | solution.py:423
  20.9 4.3 %collective-permute-start.2 = (f32[30,4,128]{2,1,0:T(4,128)S(1)}, f32[30,4,128]{2,1,0:T(4,128)S(1)}, u32[]{:S(2)}, u32[]{:S(2)}) collective-permute-start(f32[30,4,128]{2,1,0:T(4,128)S(1)} %get-tuple-element.14), channel_id=1, source_target_pairs={{0,4},{4,0},{1,5},{5,1},{2,6},{6,2},{3,7},{7,3},{8,12},{12,8},{9,1... | collective-permute-start | bytes 184328 | tf_op jit(solution)/shard_map/ppermute | solution.py:425
  22.5 4.2 %collective-permute-start.3 = (f32[30,4,128]{2,1,0:T(4,128)S(1)}, f32[30,4,128]{2,1,0:T(4,128)S(1)}, u32[]{:S(2)}, u32[]{:S(2)}) collective-permute-start(f32[30,4,128]{2,1,0:T(4,128)S(1)} %get-tuple-element.15), channel_id=1, source_target_pairs={{0,1},{1,0},{2,3},{3,2},{4,5},{5,4},{6,7},{7,6},{8,9},{9,8},{10,11... | collective-permute-start | bytes 184328 | tf_op jit(solution)/shard_map/ppermute | solution.py:426
  23.0 5.1 %collective-permute-start.4 = (f32[30,4,128]{2,1,0:T(4,128)S(1)}, f32[30,4,128]{2,1,0:T(4,128)S(1)}, u32[]{:S(2)}, u32[]{:S(2)}) collective-permute-start(f32[30,4,128]{2,1,0:T(4,128)S(1)} %get-tuple-element.16), channel_id=1, source_target_pairs={{0,5},{1,4},{2,7},{3,6},{4,1},{5,0},{6,3},{7,2},{8,13},{9,12},{10,... | collective-permute-start | bytes 184328 | tf_op jit(solution)/shard_map/ppermute | solution.py:427
  28.2 6.3 %collective-permute-start.5 = (f32[4,30,4,128]{3,2,1,0:T(4,128)S(1)}, f32[4,30,4,128]{3,2,1,0:T(4,128)S(1)}, u32[]{:S(2)}, u32[]{:S(2)}) collective-permute-start(f32[4,30,4,128]{3,2,1,0:T(4,128)S(1)} %pad_maximum_fusion.own_ref), channel_id=1, source_target_pairs={{0,16},{8,24},{16,0},{24,8},{1,17},{9,25},{17,1},{25,9},{2,18},{10... | collective-permute-start | bytes 737288 | tf_op jit(solution)/shard_map/ppermute | solution.py:429
  29.7 4.7 %collective-permute-start.6 = (f32[4,30,4,128]{3,2,1,0:T(4,128)S(1)}, f32[4,30,4,128]{3,2,1,0:T(4,128)S(1)}, u32[]{:S(2)}, u32[]{:S(2)}) collective-permute-start(f32[4,30,4,128]{3,2,1,0:T(4,128)S(1)} %pad_maximum_fusion.own_ref), channel_id=1, source_target_pairs={{0,8},{8,0},{16,24},{24,16},{1,9},{9,1},{17,25},{25,17},{2,10},{10... | collective-permute-start | bytes 737288 | tf_op jit(solution)/shard_map/ppermute | solution.py:430
  34.4 1.5 %collective-permute-start.7 = (f32[4,30,4,128]{3,2,1,0:T(4,128)S(1)}, f32[4,30,4,128]{3,2,1,0:T(4,128)S(1)}, u32[]{:S(2)}, u32[]{:S(2)}) collective-permute-start(f32[4,30,4,128]{3,2,1,0:T(4,128)S(1)} %collective-permute-done.5.across_ref), channel_id=1, source_target_pairs={{0,8},{8,0},{16,24},{24,16},{1,9},{9,1},{17,25},{25,17},{2,10},{10... | collective-permute-start | bytes 737288 | tf_op jit(solution)/shard_map/ppermute | solution.py:431
